TPU v7x, 256 devices: a whole 4x4x8 slice. The times are simulated.
256 devices in a mesh: ctx: 32 (over x, y, core), head: 8 (over z).
Axes of the slice: x: 4, y: 4, z: 8, core: 2. Of those that a mesh axis runs over, the one named last changes fastest.
Arguments:
- queries: bfloat16 [8192, 2048], P(('ctx', 'head')), may hold values from -6 to 6
- keys: bfloat16 [8192, 2048], P(('ctx', 'head')), may hold values from -6 to 6
- values: bfloat16 [8192, 2048], P(('ctx', 'head')), may hold values from -6 to 6
- ridge: float32 [16], P('head'), may hold values from 0.5 to 4
- gain: float32 [2048], P('head'), may hold values from 0.5 to 1.5
Outputs:
- mixed: bfloat16 [8192, 2048], P(('ctx', 'head'))
All inputs are finite; a program needn't handle non-finite values.
Results may differ from a plain program's by a relative error of at most 0.0015.
Values may be sent and summed in bfloat16 or wider, within the bound.
No kernel may reach another device: no remote copies, remote signals or barrier semaphores. Data moves between devices by JAX's collectives and lax.ppermute only.
A program may use at most 64 MiB of HBM per device.

v0:
```python
import jax
import jax.numpy as jnp
from jax import lax
from jax.sharding import Mesh
from jax.sharding import PartitionSpec as P

ITERS = 4
CTX = ("ctx_0", "ctx_1", "ctx_2")
CTX_HEAD = ("ctx_0", "ctx_1", "ctx_2", "head")


EPS = 1e-06
HIGH = lax.Precision.HIGHEST


def nothing_yet(value, identity):
    return jax.tree.map(
        lambda part, zero: jnp.zeros_like(part) + jnp.asarray(zero, part.dtype), value, identity
    )


def prefix_by_axis(value, axes, combine, identity):
    before = start = nothing_yet(value, identity)
    so_far = value
    for axis in reversed(axes):
        count, position = (lax.axis_size(axis), lax.axis_index(axis))
        pieces = jax.tree.map(lambda part: lax.all_gather(part, axis), so_far)
        inside, so_far = (start, start)
        for k in range(count):
            passed = k < position
            so_far = combine(so_far, jax.tree.map(lambda part: part[k], pieces))
            inside = jax.tree.map(lambda new, old: jnp.where(passed, new, old), so_far, inside)
        before = combine(inside, before)
    return before


def unit_rows(matrix):
    return matrix * lax.rsqrt(jnp.sum(matrix * matrix, -1, keepdims=True) + EPS)


def add_states(earlier, later):
    return (earlier[0] + later[0], earlier[1] + later[1])


def on_device(queries, keys, values, ridge, gain):
    arrived = (
        lax.all_to_all(queries, "head", split_axis=1, concat_axis=0, tiled=True),
        lax.all_to_all(keys, "head", split_axis=1, concat_axis=0, tiled=True),
        lax.all_to_all(values, "head", split_axis=1, concat_axis=0, tiled=True),
    )
    local_heads = ridge.shape[0]
    rows = arrived[0].shape[0]
    width = arrived[0].shape[1] // local_heads

    def to_heads(matrix):
        return matrix.astype(jnp.float32).reshape(rows, local_heads, width).transpose(1, 0, 2)

    query_h = unit_rows(to_heads(arrived[0]))
    key_h = unit_rows(to_heads(arrived[1]))
    value_h = to_heads(arrived[2])
    key_local = jnp.einsum("hld,hle->hde", key_h, key_h, precision=HIGH)
    value_local = jnp.einsum("hld,hle->hde", value_h, key_h, precision=HIGH)
    empty = jnp.zeros_like(key_local)
    key_state, value_state = prefix_by_axis(
        (key_local, value_local), CTX, add_states, (empty, empty)
    )
    causal = jnp.tril(jnp.ones((rows, rows), jnp.float32))
    strength = ridge.reshape(local_heads, 1, 1)
    answer = jnp.zeros_like(query_h)
    resid = query_h
    direction = query_h
    rr_now = jnp.sum(resid * resid, -1, keepdims=True)
    for turn in range(ITERS):
        apply_scores = jnp.einsum("htd,hid->hti", direction, key_h, precision=HIGH) * causal
        image = (
            jnp.einsum("hti,hid->htd", apply_scores, key_h, precision=HIGH)
            + jnp.einsum("htd,hde->hte", direction, key_state, precision=HIGH)
            + strength * direction
        )
        alpha = rr_now / (jnp.sum(direction * image, -1, keepdims=True) + EPS)
        answer = answer + alpha * direction
        resid = resid - alpha * image
        rr_next = jnp.sum(resid * resid, -1, keepdims=True)
        direction = resid + rr_next / (rr_now + EPS) * direction
        rr_now = rr_next
    scores = jnp.einsum("htd,hid->hti", answer, key_h, precision=HIGH) * causal
    readout = jnp.einsum("hti,hid->htd", scores, value_h, precision=HIGH) + jnp.einsum(
        "hte,hde->htd", answer, value_state, precision=HIGH
    )
    scale = lax.rsqrt(jnp.mean(readout * readout, -1, keepdims=True) + EPS)
    normed = readout * scale * gain.reshape(local_heads, 1, width)
    outgoing = normed.transpose(1, 0, 2).reshape(rows, local_heads * width).astype(jnp.bfloat16)
    return lax.all_to_all(outgoing, "head", split_axis=0, concat_axis=1, tiled=True)


def solution(mesh):
    split = Mesh(
        mesh.devices.reshape(4, 4, 2, mesh.shape["head"]), ("ctx_0", "ctx_1", "ctx_2", "head")
    )
    in_specs = (P(CTX_HEAD, None), P(CTX_HEAD, None), P(CTX_HEAD, None), P("head"), P("head"))
    out_specs = P(CTX_HEAD, None)
    return jax.shard_map(
        on_device, mesh=split, in_specs=in_specs, out_specs=out_specs, check_vma=False
    )
```

profile of v0, /device:TPU:8, one launch (start us, length us, event | category | flops | bytes accessed | tf_op | source)
XLA Modules:
  0.0 118.2 jit_solution(7779742252768618925)
XLA Ops:
  0.0 1.5 %copy.241 = bf16[4,8,8,256]{3,2,0,1:T(8,128)(2,1)} copy(bf16[4,8,8,256]{3,2,1,0:T(8,128)(2,1)} %bitcast.137) | data formatting | bytes 262144 | tf_op jit(solution)/shard_map/all_to_all | solution.py:48
  1.6 8.6 %all-to-all-start.1 = ((bf16[32,8,256]{2,0,1:T(8,128)(2,1)}), bf16[32,8,256]{2,0,1:T(8,128)(2,1)S(1)}, u32[]{:S(2)}, u32[]{:S(2)}) async-start(bf16[32,8,256]{2,0,1:T(8,128)(2,1)} %bitcast.133), calls=%async_computation.1 | async-start | bytes 262144 | tf_op jit(solution)/shard_map/all_to_all | solution.py:48
  10.2 0.7 copy.242
  10.8 0.3 copy-done.1
  11.1 0.7 copy.240
  11.8 7.5 %all-to-all-done.1 = bf16[32,8,256]{2,0,1:T(8,128)(2,1)S(1)} async-done(((bf16[32,8,256]{2,0,1:T(8,128)(2,1)}), bf16[32,8,256]{2,0,1:T(8,128)(2,1)S(1)}, u32[]{:S(2)}, u32[]{:S(2)}) %all-to-all-start.1) | async-done | bytes 131104 | tf_op jit(solution)/shard_map/all_to_all | solution.py:48
  19.2 3.4 %all-to-all-start = ((bf16[32,8,256]{2,0,1:T(8,128)(2,1)}), bf16[32,8,256]{2,0,1:T(8,128)(2,1)S(1)}, u32[]{:S(2)}, u32[]{:S(2)}) async-start(bf16[32,8,256]{2,0,1:T(8,128)(2,1)} %bitcast.134), calls=%async_computation | async-start | bytes 262144 | tf_op jit(solution)/shard_map/all_to_all | solution.py:47
  22.7 0.1 reshape.181
  22.8 0.1 fusion.8
  23.0 0.8 fusion.52
  23.7 2.0 %all-gather = f32[4,128,128]{2,1,0:T(8,128)S(1)} all-gather(f32[2,128,128]{2,1,0:T(8,128)S(1)} %fusion.52), channel_id=2, replica_groups=mesh['ctx_0'=4,'ctx_1'=4,'ctx_2'=2,'head'=8] {'ctx_2'}, dimensions={0}, use_global_device_ids=true | all-gather | bytes 393216 | tf_op jit(solution)/shard_map/all_gather | solution.py:27
  25.7 13.5 %all-gather.2 = f32[8,128,128]{2,1,0:T(8,128)S(1)} all-gather(f32[2,128,128]{2,1,0:T(8,128)S(1)} %slice_add_fusion.13), channel_id=4, replica_groups=mesh['ctx_0'=4,'ctx_1'=4,'ctx_2'=2,'head'=8] {'ctx_1'}, dimensions={0}, use_global_device_ids=true | all-gather | bytes 655360 | tf_op jit(solution)/shard_map/all_gather | solution.py:27
  39.3 13.2 %all_gather.31 = f32[4,2,128,128]{3,2,1,0:T(8,128)S(1)} all-gather(f32[1,2,128,128]{3,2,1,0:T(8,128)S(1)} %fusion.19), channel_id=1, replica_groups=mesh['ctx_0'=4,'ctx_1'=4,'ctx_2'=2,'head'=8] {'ctx_0'}, dimensions={0}, use_global_device_ids=true | all-gather | bytes 655360 | tf_op jit(solution)/shard_map/all_gather | solution.py:27
  52.5 7.4 %all-to-all-start.2 = ((bf16[32,8,256]{2,0,1:T(8,128)(2,1)}), bf16[32,8,256]{2,0,1:T(8,128)(2,1)S(1)}, u32[]{:S(2)}, u32[]{:S(2)}) async-start(bf16[32,8,256]{2,0,1:T(8,128)(2,1)} %bitcast.132), calls=%async_computation.2 | async-start | bytes 262144 | tf_op jit(solution)/shard_map/all_to_all | solution.py:49
  59.9 0.1 reshape.180
  60.1 0.1 copy.165
  60.3 0.7 convolution_multiply_fusion.4
  61.0 0.8 fusion.53
  61.8 0.1 fusion.18
  61.9 0.5 copy-done.2
  62.5 0.5 multiply_reduce_fusion.6
  63.0 0.1 multiply_reduce_fusion.5
  63.1 0.7 convolution_multiply_fusion.3
  63.8 0.8 fusion.51
  64.7 0.5 multiply_reduce_fusion.4
  65.1 0.1 multiply_reduce_fusion.3
  65.3 0.7 convolution_multiply_fusion.2
  66.0 0.8 fusion.50
  66.8 0.5 multiply_reduce_fusion.2
  67.5 0.7 convolution_multiply_fusion.1
  68.2 0.8 fusion.49
  69.0 0.5 fusion.5
  69.5 0.1 multiply_add_fusion
  69.6 0.7 convolution_multiply_fusion
  70.3 0.1 copy.189
  70.5 0.5 convolution_bitcast_fusion
  71.0 0.4 fusion.21
  71.4 0.1 copy.192
  71.5 2.0 %all-gather.1 = f32[4,128,128]{2,1,0:T(8,128)S(1)} all-gather(f32[2,128,128]{2,1,0:T(8,128)S(1)} %copy.192), channel_id=3, replica_groups=mesh['ctx_0'=4,'ctx_1'=4,'ctx_2'=2,'head'=8] {'ctx_2'}, dimensions={0}, use_global_device_ids=true | all-gather | bytes 393216 | tf_op jit(solution)/shard_map/all_gather | solution.py:27
  73.5 13.4 %all-gather.3 = f32[8,128,128]{2,1,0:T(8,128)S(1)} all-gather(f32[2,128,128]{2,1,0:T(8,128)S(1)} %slice_add_fusion.6), channel_id=5, replica_groups=mesh['ctx_0'=4,'ctx_1'=4,'ctx_2'=2,'head'=8] {'ctx_1'}, dimensions={0}, use_global_device_ids=true | all-gather | bytes 655360 | tf_op jit(solution)/shard_map/all_gather | solution.py:27
  87.0 13.0 %all_gather.35 = f32[4,2,128,128]{3,2,1,0:T(8,128)S(1)} all-gather(f32[1,2,128,128]{3,2,1,0:T(8,128)S(1)} %fusion.15), channel_id=1, replica_groups=mesh['ctx_0'=4,'ctx_1'=4,'ctx_2'=2,'head'=8] {'ctx_0'}, dimensions={0}, use_global_device_ids=true | all-gather | bytes 655360 | tf_op jit(solution)/shard_map/all_gather | solution.py:27
  100.0 0.5 multiply_reduce_fusion
  100.5 0.7 copy-done.3
  101.2 0.1 fusion.7
  101.3 0.1 copy.194
  101.4 0.1 convert_element_type.29
  101.5 16.1 %all_to_all.58 = bf16[8,32,256]{2,1,0:T(8,128)(2,1)S(1)} all-to-all(bf16[8,32,256]{2,1,0:T(8,128)(2,1)S(1)} %convert_element_type.29), channel_id=1, replica_groups=mesh['ctx_0'=4,'ctx_1'=4,'ctx_2'=2,'head'=8] {'head'}, dimensions={0} | all-to-all | bytes 262144 | tf_op jit(solution)/shard_map/all_to_all | solution.py:93
  117.6 0.7 copy.223
  (30 shorter events, 0.5 us)
Async XLA Ops:
  1.6 8.6 %copy-start = (bf16[32,2048]{1,0:T(8,128)(2,1)S(1)}, bf16[32,2048]{1,0:T(8,128)(2,1)}, u32[]{:S(2)}) copy-start(bf16[32,2048]{1,0:T(8,128)(2,1)} %param.5) | copy-start | bytes 393220
  1.6 17.7 %all-to-all-start.1 = ((bf16[32,8,256]{2,0,1:T(8,128)(2,1)}), bf16[32,8,256]{2,0,1:T(8,128)(2,1)S(1)}, u32[]{:S(2)}, u32[]{:S(2)}) async-start(bf16[32,8,256]{2,0,1:T(8,128)(2,1)} %bitcast.133), calls=%async_computation.1 | async-start | bytes 262144 | tf_op jit(solution)/shard_map/all_to_all | solution.py:48
  10.2 1.0 copy-start.1
  19.2 33.2 %all-to-all-start = ((bf16[32,8,256]{2,0,1:T(8,128)(2,1)}), bf16[32,8,256]{2,0,1:T(8,128)(2,1)S(1)}, u32[]{:S(2)}, u32[]{:S(2)}) async-start(bf16[32,8,256]{2,0,1:T(8,128)(2,1)} %bitcast.134), calls=%async_computation | async-start | bytes 262144 | tf_op jit(solution)/shard_map/all_to_all | solution.py:47
  52.5 17.8 %all-to-all-start.2 = ((bf16[32,8,256]{2,0,1:T(8,128)(2,1)}), bf16[32,8,256]{2,0,1:T(8,128)(2,1)S(1)}, u32[]{:S(2)}, u32[]{:S(2)}) async-start(bf16[32,8,256]{2,0,1:T(8,128)(2,1)} %bitcast.132), calls=%async_computation.2 | async-start | bytes 262144 | tf_op jit(solution)/shard_map/all_to_all | solution.py:49
  61.8 0.7 copy-start.2
  100.5 0.7 copy-start.3
where the time goes:
time: 119 us; the launch traced here: 118 us
  blocking collectives  73.1 us (61%)
  starting transfers between devices  19.4 us (16%)
  matrix products  10.9 us (9%)
  waiting for transfers between devices  7.46 us (6%)
  local copies, waits for them, and re-layouts  5.91 us (5%)
    all_gather x6, blocking collectives, prefix_by_axis(): pieces = jax.tree.map(lambda part: lax.all_gather(part, axis), so_far)  57.1 us
    all_to_all x1, blocking collectives, on_device(): lax.all_to_all(outgoing, 'head', split_axis=0, concat_axis=1, tiled=True)  16.1 us
    all_to_all x1, starting transfers between devices, on_device(): lax.all_to_all(keys, 'head', split_axis=1, concat_axis=0, tiled=True)  8.6 us
    all_to_all x1, waiting for transfers between devices, on_device(): lax.all_to_all(keys, 'head', split_axis=1, concat_axis=0, tiled=True)  7.45 us
    all_to_all x1, starting transfers between devices, on_device(): lax.all_to_all(values, 'head', split_axis=1, concat_axis=0, tiled=True)  7.44 us
    all_to_all x1, starting transfers between devices, on_device(): lax.all_to_all(queries, 'head', split_axis=1, concat_axis=0, tiled=True)  3.37 us
    dot_general x4, matrix products, on_device(): jnp.einsum('hti,hid->htd', apply_scores, key_h, precision=HIGH)  3.24 us
    dot_general x4, matrix products, on_device(): jnp.einsum('htd,hid->hti', direction, key_h, precision=HIGH) * causal  2.89 us
  transfers between devices with their start and end apart: 3, of which 1 were waited for; matrix products, arithmetic and copies ran while one was open for 10% of the time, Pallas kernels for 0%

commit v1 on v0

v1 whole, which is shorter than its diff:
```python
import jax
import jax.numpy as jnp
from jax import lax
from jax.sharding import Mesh
from jax.sharding import PartitionSpec as P

ITERS = 4
CTX_HEAD = ("x", "y", "core", "head")
PEERS = ("head", "core")


EPS = 1e-06
HIGH = lax.Precision.HIGHEST


def unit_rows(matrix):
    return matrix * lax.rsqrt(jnp.sum(matrix * matrix, -1, keepdims=True) + EPS)


def earlier_states(local):
    x, y = lax.axis_index("x"), lax.axis_index("y")
    n_x, n_y = lax.axis_size("x"), lax.axis_size("y")
    slots = (n_x,) + local.shape
    arrived = lax.all_to_all(jnp.broadcast_to(local, slots), "x", 0, 0, tiled=True)
    ranks = jnp.arange(n_x).reshape(n_x, 1, 1)
    column = jnp.sum(jnp.where(ranks < x, arrived, 0.0), 0)
    ranks = jnp.arange(n_y).reshape(n_y, 1, 1)
    outgoing = column + jnp.where(ranks > y, local, 0.0)
    return jnp.sum(lax.all_to_all(outgoing, "y", 0, 0, tiled=True), 0)


def on_device(queries, keys, values, ridge, gain):
    rows, columns = queries.shape
    peers = lax.axis_size("head") * lax.axis_size("core")
    width = columns // peers
    packed = jnp.stack([queries, keys, values], 0).reshape(3, rows, peers, width)
    packed = packed.transpose(2, 0, 1, 3)
    arrived = lax.all_to_all(packed, PEERS, 0, 0, tiled=True)
    arrived = arrived.reshape(peers // 2, 2, 3, rows, width).transpose(2, 1, 0, 3, 4)
    arrived = arrived.reshape(3, 2, rows * peers // 2, width).astype(jnp.float32)
    core = lax.axis_index("core")
    strength = lax.dynamic_slice(ridge, (core,), (1,)).reshape(1, 1, 1)
    gain_h = lax.dynamic_slice(gain.reshape(2, width), (core, 0), (1, width)).reshape(1, 1, width)

    query_h = unit_rows(arrived[0])
    key_h = unit_rows(arrived[1])
    value_h = arrived[2]
    tokens = query_h.shape[1]
    both = jnp.concatenate([key_h, value_h], -1)
    local = jnp.einsum("hld,hle->hed", key_h, both, precision=HIGH)
    before = earlier_states(local[0] + local[1])
    state = jnp.stack([before, before + local[0]], 0)
    key_state = state[:, :width]
    value_state = state[:, width:]
    causal = jnp.tril(jnp.ones((tokens, tokens), jnp.float32))
    answer = jnp.zeros_like(query_h)
    resid = query_h
    direction = query_h
    rr_now = jnp.sum(resid * resid, -1, keepdims=True)
    for turn in range(ITERS):
        apply_scores = jnp.einsum("htd,hid->hti", direction, key_h, precision=HIGH) * causal
        image = (
            jnp.einsum("hti,hid->htd", apply_scores, key_h, precision=HIGH)
            + jnp.einsum("htd,hde->hte", direction, key_state, precision=HIGH)
            + strength * direction
        )
        alpha = rr_now / (jnp.sum(direction * image, -1, keepdims=True) + EPS)
        answer = answer + alpha * direction
        resid = resid - alpha * image
        rr_next = jnp.sum(resid * resid, -1, keepdims=True)
        direction = resid + rr_next / (rr_now + EPS) * direction
        rr_now = rr_next
    scores = jnp.einsum("htd,hid->hti", answer, key_h, precision=HIGH) * causal
    readout = jnp.einsum("hti,hid->htd", scores, value_h, precision=HIGH) + jnp.einsum(
        "hte,hde->htd", answer, value_state, precision=HIGH
    )
    scale = lax.rsqrt(jnp.mean(readout * readout, -1, keepdims=True) + EPS)
    normed = (readout * scale * gain_h).astype(jnp.bfloat16)
    outgoing = normed.reshape(2, peers // 2, rows, width).transpose(1, 0, 2, 3)
    outgoing = outgoing.reshape(peers, rows, width)
    home = lax.all_to_all(outgoing, PEERS, 0, 0, tiled=True)
    return home.transpose(1, 0, 2).reshape(rows, columns)


def solution(mesh):
    split = Mesh(mesh.devices.reshape(4, 4, 2, mesh.shape["head"]), CTX_HEAD)
    rows = P(CTX_HEAD, None)
    return jax.shard_map(
        on_device,
        mesh=split,
        in_specs=(rows, rows, rows, P("head"), P("head")),
        out_specs=rows,
        check_vma=False,
    )
```

time: 119 us -> 82.7 us (0.69)
  the two profiles are of different devices: /device:TPU:8 before, /device:TPU:1 now
where the time goes in v1:
time: 82.7 us; the launch traced here: 82.3 us
  waiting for transfers between devices  30.4 us (37%)
  starting transfers between devices  18.2 us (22%)
  blocking collectives  13.2 us (16%)
  matrix products  12.1 us (15%)
  local copies, waits for them, and re-layouts  6.01 us (7%)
  other arithmetic  2.1 us (3%)
    all_to_all x1, waiting for transfers between devices, on_device(): arrived = lax.all_to_all(packed, PEERS, 0, 0, tiled=True)  14.5 us
    all_to_all x1, blocking collectives, on_device(): home = lax.all_to_all(outgoing, PEERS, 0, 0, tiled=True)  13.2 us
    all_to_all x1, starting transfers between devices, on_device(): arrived = lax.all_to_all(packed, PEERS, 0, 0, tiled=True)  9.98 us
    all_to_all x1, waiting for transfers between devices, earlier_states(): lax.all_to_all(jnp.broadcast_to(local, slots), 'x', 0, 0, tiled=True)  8.39 us
    all_to_all x1, waiting for transfers between devices, earlier_states(): return jnp.sum(lax.all_to_all(outgoing, 'y', 0, 0, tiled=True), 0)  7.56 us
    dot_general x4, matrix products, on_device(): jnp.einsum('htd,hde->hte', direction, key_state, precision=HIGH)  4.48 us
    all_to_all x1, starting transfers between devices, earlier_states(): return jnp.sum(lax.all_to_all(outgoing, 'y', 0, 0, tiled=True), 0)  4.18 us
    all_to_all x1, starting transfers between devices, earlier_states(): lax.all_to_all(jnp.broadcast_to(local, slots), 'x', 0, 0, tiled=True)  4.01 us
  transfers between devices with their start and end apart: 3, of which 3 were waited for; matrix products, arithmetic and copies ran while one was open for 3% of the time, Pallas kernels for 0%

profile of v1, /device:TPU:1, one launch (start us, length us, event | category | flops | bytes accessed | tf_op | source)
XLA Modules:
  0.0 82.3 jit_solution(15809991187715802281)
XLA Ops:
  0.0 0.0 copy-start
  0.0 0.0 copy-start.1
  0.0 1.0 %copy.146 = bf16[4,8,16,128]{3,2,1,0:T(8,128)(2,1)S(1)} copy(bf16[4,8,16,128]{3,1,2,0:T(8,128)(2,1)} %bitcast.80) | data formatting | bytes 262144
  1.0 0.0 copy-done.1
  1.0 0.9 %copy-done.2 = bf16[32,2048]{1,0:T(8,128)(2,1)S(1)} copy-done((bf16[32,2048]{1,0:T(8,128)(2,1)S(1)}, bf16[32,2048]{1,0:T(8,128)(2,1)}, u32[]{:S(2)}) %copy-start.2) | copy-done | bytes 131096
  2.0 0.8 %copy.95 = bf16[16,3,32,128]{3,2,1,0:T(8,128)(2,1)} copy(bf16[16,3,32,128]{3,0,2,1:T(8,128)(2,1)S(1)} %maximum_bitcast_fusion) | data formatting | bytes 786432 | tf_op jit(solution)/shard_map/transpose | solution.py:37
  2.8 10.0 %all-to-all-start = ((bf16[16,3,32,128]{3,2,1,0:T(8,128)(2,1)}), bf16[16,3,32,128]{3,2,1,0:T(8,128)(2,1)S(1)}, u32[]{:S(2)}, u32[]{:S(2)}) async-start(bf16[16,3,32,128]{3,2,1,0:T(8,128)(2,1)} %copy.95), calls=%async_computation | async-start | bytes 786432 | tf_op jit(solution)/shard_map/all_to_all | solution.py:38
  12.8 14.5 %all-to-all-done = bf16[16,3,32,128]{3,2,1,0:T(8,128)(2,1)S(1)} async-done(((bf16[16,3,32,128]{3,2,1,0:T(8,128)(2,1)}), bf16[16,3,32,128]{3,2,1,0:T(8,128)(2,1)S(1)}, u32[]{:S(2)}, u32[]{:S(2)}) %all-to-all-start) | async-done | bytes 393248 | tf_op jit(solution)/shard_map/all_to_all | solution.py:38
  27.3 0.1 fusion.20
  27.5 0.1 multiply_reduce_fusion.7
  27.6 0.1 copy.99
  27.8 0.1 copy.103
  27.9 0.6 fusion.6
  28.6 0.8 %broadcast_in_dim.35 = f32[4,256,128]{2,1,0:T(8,128)} broadcast(f32[256,128]{1,0:T(8,128)S(1)} %fusion.15), dimensions={1,2} | broadcast | bytes 655360 | tf_op jit(solution)/shard_map/broadcast_in_dim | solution.py:24
  29.4 4.0 %all-to-all-start.1 = ((f32[4,256,128]{2,1,0:T(8,128)}), f32[4,256,128]{2,1,0:T(8,128)S(1)}, u32[]{:S(2)}, u32[]{:S(2)}) async-start(f32[4,256,128]{2,1,0:T(8,128)} %broadcast_in_dim.35), calls=%async_computation.1 | async-start | bytes 1048576 | tf_op jit(solution)/shard_map/all_to_all | solution.py:24
  33.4 0.0 copy-done
  33.4 0.6 copy-done.3
  34.1 0.6 dynamic_slice.6
  34.7 0.1 copy.97
  34.8 0.1 multiply_reduce_fusion.9
  35.0 8.4 %all-to-all-done.1 = f32[4,256,128]{2,1,0:T(8,128)S(1)} async-done(((f32[4,256,128]{2,1,0:T(8,128)}), f32[4,256,128]{2,1,0:T(8,128)S(1)}, u32[]{:S(2)}, u32[]{:S(2)}) %all-to-all-start.1) | async-done | bytes 524320 | tf_op jit(solution)/shard_map/all_to_all | solution.py:24
  43.4 0.1 select_reduce_fusion
  43.5 0.9 %select_add_fusion = f32[4,256,128]{2,1,0:T(8,128)} fusion(f32[256,128]{1,0:T(8,128)S(1)} %select_reduce_fusion, f32[256,128]{1,0:T(8,128)S(1)} %fusion.15, pred[4]{0:T(512)(128)(4,1)S(1)} %iota_compare_fusion.1), kind=kLoop, calls=%fused_computation.20 | loop fusion | flops 262144 | bytes 786436 | tf_op jit(solution)/shard_map/add | solution.py:28
  44.4 4.2 %all-to-all-start.2 = ((f32[4,256,128]{2,1,0:T(8,128)}), f32[4,256,128]{2,1,0:T(8,128)S(1)}, u32[]{:S(2)}, u32[]{:S(2)}) async-start(f32[4,256,128]{2,1,0:T(8,128)} %select_add_fusion), calls=%async_computation.2 | async-start | bytes 1048576 | tf_op jit(solution)/shard_map/all_to_all | solution.py:29
  48.6 0.6 convolution_multiply_fusion.4
  49.2 0.7 fusion.21
  49.9 7.6 %all-to-all-done.2 = f32[4,256,128]{2,1,0:T(8,128)S(1)} async-done(((f32[4,256,128]{2,1,0:T(8,128)}), f32[4,256,128]{2,1,0:T(8,128)S(1)}, u32[]{:S(2)}, u32[]{:S(2)}) %all-to-all-start.2) | async-done | bytes 524320 | tf_op jit(solution)/shard_map/all_to_all | solution.py:29
  57.5 1.1 %multiply_reduce_fusion.6 = (f32[2,256]{1,0:T(2,128)S(1)}, f32[2,256]{1,0:T(2,128)S(1)}, f32[2,256,128]{1,2,0:T(8,128)S(1)}) fusion(f32[2,256,128]{1,2,0:T(8,128)S(1)} %copy.97, f32[2,256]{1,0:T(2,128)S(1)} %add_rsqrt_fusion.2, f32[]{:T(128)} %bitcast.8, f32[2,256,128]{1,2,0:T(8,128)S(1)} %fusion.21, f32[2,128,128]{2,1,0:T(8,128)S(1)} %fusion.13), kind=kOutput, calls=%fused_computation.39 | convolution fusion | flops 101252096 | bytes 923652 | tf_op jit(solution)/shard_map/htd,hde->hte/dot_general | solution.py:64
  58.7 0.1 multiply_reduce_fusion.5
  58.8 0.6 convolution_multiply_fusion.3
  59.5 0.7 fusion.22
  60.2 1.1 %multiply_reduce_fusion.4 = (f32[2,256]{1,0:T(2,128)S(1)}, f32[2,256,128]{1,2,0:T(8,128)S(1)}) fusion(f32[2,256,128]{1,2,0:T(8,128)S(1)} %multiply_add_fusion.3, f32[]{:T(128)} %bitcast.8, f32[2,256,128]{1,2,0:T(8,128)S(1)} %fusion.22, f32[2,128,128]{2,1,0:T(8,128)S(1)} %fusion.13), kind=kOutput, calls=%fused_computation.35 | convolution fusion | flops 100990464 | bytes 919556 | tf_op jit(solution)/shard_map/htd,hde->hte/dot_general | solution.py:64
  61.3 0.1 multiply_reduce_fusion.3
  61.4 0.6 convolution_multiply_fusion.2
  62.1 0.7 fusion.23
  62.8 1.1 %multiply_reduce_fusion.2 = (f32[2,256]{1,0:T(2,128)S(1)}, f32[2,256,128]{1,2,0:T(8,128)S(1)}) fusion(f32[2,256,128]{1,2,0:T(8,128)S(1)} %multiply_add_fusion.2, f32[]{:T(128)} %bitcast.8, f32[2,256,128]{1,2,0:T(8,128)S(1)} %fusion.23, f32[2,128,128]{2,1,0:T(8,128)S(1)} %fusion.13), kind=kOutput, calls=%fused_computation.31 | convolution fusion | flops 100990464 | bytes 919556 | tf_op jit(solution)/shard_map/htd,hde->hte/dot_general | solution.py:64
  63.9 0.1 multiply_reduce_fusion.1
  64.0 0.1 multiply_add_fusion.1
  64.1 0.6 convolution_multiply_fusion.1
  64.7 0.7 fusion.24
  65.4 1.1 %fusion.5 = f32[2,256]{1,0:T(2,128)S(1)} fusion(f32[2,256,128]{1,2,0:T(8,128)S(1)} %multiply_add_fusion.1, f32[2,256,128]{1,2,0:T(8,128)S(1)} %fusion.24, f32[2,128,128]{2,1,0:T(8,128)S(1)} %fusion.13, f32[]{:T(128)} %bitcast.8), kind=kOutput, calls=%fused_computation.15 | convolution fusion | flops 100990464 | bytes 657412 | tf_op jit(solution)/shard_map/htd,hde->hte/dot_general | solution.py:64
  66.5 0.1 multiply_add_fusion
  66.6 0.6 convolution_multiply_fusion
  67.2 0.4 fusion.25
  67.6 0.7 multiply_reduce_fusion
  68.3 0.1 multiply_convert_fusion
  68.5 13.2 %all_to_all.20 = bf16[16,32,128]{2,1,0:T(8,128)(2,1)S(1)} all-to-all(bf16[16,32,128]{2,1,0:T(8,128)(2,1)S(1)} %bitcast.76), channel_id=1, replica_groups=mesh['x'=4,'y'=4,'core'=2,'head'=8] {'head','core'}, dimensions={0} | all-to-all | bytes 262144 | tf_op jit(solution)/shard_map/all_to_all | solution.py:81
  81.7 0.7 copy_bitcast_fusion
  (32 shorter events, 0.5 us)
Async XLA Ops:
  0.0 33.4 %copy-start = (f32[256]{0:T(256)S(1)}, f32[256]{0:T(256)}, u32[]{:S(2)}) copy-start(f32[256]{0:T(256)} %param.9) | copy-start | bytes 3076
  0.0 1.0 %copy-start.1 = (bf16[32,2048]{1,0:T(8,128)(2,1)S(1)}, bf16[32,2048]{1,0:T(8,128)(2,1)}, u32[]{:S(2)}) copy-start(bf16[32,2048]{1,0:T(8,128)(2,1)} %param.6) | copy-start | bytes 393220
  1.0 0.9 %copy-start.2 = (bf16[32,2048]{1,0:T(8,128)(2,1)S(1)}, bf16[32,2048]{1,0:T(8,128)(2,1)}, u32[]{:S(2)}) copy-start(bf16[32,2048]{1,0:T(8,128)(2,1)} %param.7) | copy-start | bytes 393220
  2.8 24.5 %all-to-all-start = ((bf16[16,3,32,128]{3,2,1,0:T(8,128)(2,1)}), bf16[16,3,32,128]{3,2,1,0:T(8,128)(2,1)S(1)}, u32[]{:S(2)}, u32[]{:S(2)}) async-start(bf16[16,3,32,128]{3,2,1,0:T(8,128)(2,1)} %copy.95), calls=%async_computation | async-start | bytes 786432 | tf_op jit(solution)/shard_map/all_to_all | solution.py:38
  29.4 14.0 %all-to-all-start.1 = ((f32[4,256,128]{2,1,0:T(8,128)}), f32[4,256,128]{2,1,0:T(8,128)S(1)}, u32[]{:S(2)}, u32[]{:S(2)}) async-start(f32[4,256,128]{2,1,0:T(8,128)} %broadcast_in_dim.35), calls=%async_computation.1 | async-start | bytes 1048576 | tf_op jit(solution)/shard_map/all_to_all | solution.py:24
  33.4 0.7 copy-start.3
  44.4 13.1 %all-to-all-start.2 = ((f32[4,256,128]{2,1,0:T(8,128)}), f32[4,256,128]{2,1,0:T(8,128)S(1)}, u32[]{:S(2)}, u32[]{:S(2)}) async-start(f32[4,256,128]{2,1,0:T(8,128)} %select_add_fusion), calls=%async_computation.2 | async-start | bytes 1048576 | tf_op jit(solution)/shard_map/all_to_all | solution.py:29

commit v2 on v1

v2 whole, which is shorter than its diff:
```python
import functools

import jax
import jax.numpy as jnp
from jax import lax
from jax.experimental import pallas as pl
from jax.experimental.pallas import tpu as pltpu
from jax.sharding import Mesh
from jax.sharding import PartitionSpec as P

ITERS = 4
CTX_HEAD = ("x", "y", "core", "head")
PEERS = ("core", "head")
EPS = 1e-06
DH = 128
SUB = 128

VMEM = pl.BlockSpec(memory_space=pltpu.VMEM)
HBM = pl.BlockSpec(memory_space=pltpu.HBM)
SMEM = pl.BlockSpec(memory_space=pltpu.SMEM)
BF = jnp.bfloat16
F32 = jnp.float32
ROOM = pltpu.CompilerParams(vmem_limit_bytes=16 * 2**20)


def pieces(value, count):
    out = []
    for _ in range(count - 1):
        out.append(value.astype(BF))
        value = value - out[-1].astype(F32)
    return out + [value.astype(BF)]


def wide(parts):
    return jnp.concatenate(parts, 1)


def tall(parts):
    return jnp.concatenate(parts, 0)


def dot(a, b):
    return lax.dot_general(a, b, (((1,), (0,)), ((), ())), preferred_element_type=F32)


def tokens_of(arrived_ref, which, sub):
    count = SUB // arrived_ref.shape[2]
    return tall([arrived_ref[sub * count + i, which] for i in range(count)])


def squared_sum(value):
    return jnp.sum(value * value, -1, keepdims=True)


def pack_kernel(
    query_ref, key_ref, value_ref, ridge_ref, gain_ref, out_ref, head_ref, held, flags, *, peers
):
    copies = [
        pltpu.make_async_copy(ref, held.at[which], flags.at[which])
        for which, ref in enumerate((query_ref, key_ref, value_ref))
    ]
    for copy in copies:
        copy.start()
    core = lax.axis_index("core")
    head_ref[...] = jnp.full(head_ref.shape, ridge_ref[core], F32)
    head_ref[pl.ds(0, 1), :] = gain_ref[pl.ds(core, 1), :]
    half = peers // 2
    for which, copy in enumerate(copies):
        copy.wait()
        for peer in range(peers):
            head = 2 * (peer % half) + peer // half
            out_ref[peer, which] = held[which, :, head * DH : (head + 1) * DH]


def states_kernel(arrived_ref, before_ref, total_ref, *, subs):
    total = None
    for sub in range(subs):
        key = tokens_of(arrived_ref, 1, sub)
        value = tokens_of(arrived_ref, 2, sub)
        key_f = key.astype(F32)
        unit = lax.rsqrt(squared_sum(key_f) + EPS)
        right = wide([key_f * (unit * unit), value.astype(F32) * unit])
        key_t = key_f.T.astype(BF)
        state = dot(wide([key_t, key_t]), tall(pieces(right, 2)))
        total = state if total is None else total + state
        if sub + 1 < subs:
            before_ref[sub] = total
    total_ref[...] = total


def from_others(index, own, others, steps):
    total, earlier = own, None
    for step, ref in zip(steps, others):
        value = ref[...]
        total = total + value
        part = jnp.where(index >= step, value, 0.0)
        earlier = part if earlier is None else earlier + part
    return total, earlier


def row_kernel(own_ref, *refs, steps):
    total_ref, earlier_ref = refs[-2:]
    total, earlier = from_others(
        lax.axis_index("y"), own_ref[...], refs[:-2], steps
    )
    total_ref[...] = total
    earlier_ref[...] = earlier


def solve_kernel(head_ref, arrived_ref, before_ref, earlier_ref, *refs, subs, steps):
    out_ref = refs[-1]
    gain, strength = head_ref[0:1, :], head_ref[1:2, :]
    earlier = earlier_ref[...]
    _, rows_before = from_others(lax.axis_index("x"), earlier, refs[:-1], steps)
    base = earlier + rows_before
    row = lax.broadcasted_iota(jnp.int32, (SUB, SUB), 0)
    column = lax.broadcasted_iota(jnp.int32, (SUB, SUB), 1)
    causal = column <= row

    every = range(subs)
    keys, key_pair, operator, low_state, weights, units = [], [], [], [], [], []
    value_state = []
    resid, answer, direction, rr_now = [], [], [], []
    for sub in every:
        state = base if sub == 0 else base + before_ref[sub - 1]
        key = tokens_of(arrived_ref, 1, sub)
        key_f = key.astype(F32)
        unit_t = lax.rsqrt(jnp.sum((key_f * key_f).T, 0, keepdims=True) + EPS)
        units.append(jnp.where(causal, unit_t, 0.0))
        weights.append(jnp.where(causal, unit_t * unit_t, 0.0))
        high, middle, low = pieces(state[:, :DH], 3)
        key_t = key_f.T.astype(BF)
        keys.append(key_t)
        key_pair.append(tall([key, key]))
        operator.append(tall([wide([key_t, high])] * 3))
        low_state.append(tall([wide([middle, low])] * 2))
        value_state.append(state[:, DH:])
        query = tokens_of(arrived_ref, 0, sub).astype(F32)
        query = query * lax.rsqrt(squared_sum(query) + EPS)
        resid.append(query)
        direction.append(query)
        answer.append(None)
        rr_now.append(squared_sum(query))
    for turn in range(ITERS):
        parts = [wide(pieces(direction[s], 3)) for s in every]
        first = [dot(parts[s], operator[s]) for s in every]
        rest = [dot(parts[s][:, : 2 * DH], low_state[s]) for s in every]
        scores = [wide(pieces(first[s][:, :SUB] * weights[s], 2)) for s in every]
        image = [
            dot(scores[s], key_pair[s])
            + (first[s][:, SUB:] + (rest[s][:, :DH] + rest[s][:, DH:]))
            + strength * direction[s]
            for s in every
        ]
        for s in every:
            alpha = rr_now[s] / (jnp.sum(direction[s] * image[s], -1, keepdims=True) + EPS)
            step = alpha * direction[s]
            answer[s] = step if turn == 0 else answer[s] + step
            if turn + 1 < ITERS:
                resid[s] = resid[s] - alpha * image[s]
                rr_next = squared_sum(resid[s])
                direction[s] = resid[s] + rr_next / (rr_now[s] + EPS) * direction[s]
                rr_now[s] = rr_next
    rows = out_ref.shape[1]
    count = SUB // rows
    for s in every:
        high, low = pieces(value_state[s], 2)
        parts = wide(pieces(answer[s], 2))
        first = dot(parts, tall([wide([keys[s], high])] * 2))
        scores = wide(pieces(first[:, :SUB] * units[s], 2))
        value = tokens_of(arrived_ref, 2, s)
        readout = dot(scores, tall([value, value]))
        readout = readout + (first[:, SUB:] + dot(parts[:, :DH], low))
        scale = lax.rsqrt(squared_sum(readout) * (1.0 / DH) + EPS)
        normed = (readout * scale * gain).astype(BF)
        for i in range(count):
            out_ref[s * count + i] = normed[i * rows : (i + 1) * rows]


def exchange(value):
    return lax.all_to_all(value, PEERS, 0, 0, tiled=True)


def from_ring(value, axis, steps):
    size = lax.axis_size(axis)
    return [
        lax.ppermute(value, axis, [(i, (i + step) % size) for i in range(size)]) for step in steps
    ]


def ring_steps(size):
    return sorted(range(1, size), key=lambda step: min(step, size - step))


def on_device(queries, keys, values, ridge, gain):
    rows, columns = queries.shape
    half = lax.axis_size("head")
    peers = 2 * half
    n_x, n_y = lax.axis_size("x"), lax.axis_size("y")
    subs = peers * rows // SUB
    steps_x, steps_y = ring_steps(n_x), ring_steps(n_y)
    packed, head = pl.pallas_call(
        functools.partial(pack_kernel, peers=peers),
        out_shape=(
            jax.ShapeDtypeStruct((peers, 3, rows, DH), BF),
            jax.ShapeDtypeStruct((8, DH), F32),
        ),
        in_specs=[HBM, HBM, HBM, SMEM, VMEM],
        out_specs=(VMEM, VMEM),
        scratch_shapes=[
            pltpu.VMEM((3, rows, columns), BF),
            pltpu.SemaphoreType.DMA((3,)),
        ],
        compiler_params=ROOM,
        name="pack",
    )(queries, keys, values, ridge, gain.reshape(2, DH))
    arrived = exchange(packed)

    state = jax.ShapeDtypeStruct((DH, 2 * DH), F32)
    before, own = pl.pallas_call(
        functools.partial(states_kernel, subs=subs),
        out_shape=(jax.ShapeDtypeStruct((subs - 1,) + state.shape, F32), state),
        in_specs=[VMEM],
        out_specs=(VMEM, VMEM),
        compiler_params=ROOM,
        name="states",
    )(arrived)
    total, earlier = pl.pallas_call(
        functools.partial(row_kernel, steps=steps_y),
        out_shape=(state, state),
        in_specs=[VMEM] * n_y,
        out_specs=(VMEM, VMEM),
        compiler_params=ROOM,
        name="row",
    )(own, *from_ring(own, "y", steps_y))
    outgoing = pl.pallas_call(
        functools.partial(solve_kernel, subs=subs, steps=steps_x),
        out_shape=jax.ShapeDtypeStruct((peers, rows, DH), BF),
        in_specs=[VMEM] * (3 + n_x),
        out_specs=VMEM,
        compiler_params=ROOM,
        name="solve",
    )(head, arrived, before, earlier, *from_ring(total, "x", steps_x))
    home = exchange(outgoing).reshape(2, half, rows, DH)
    return home.transpose(2, 1, 0, 3).reshape(rows, columns)


def solution(mesh):
    split = Mesh(mesh.devices.reshape(4, 4, 2, mesh.shape["head"]), CTX_HEAD)
    rows = P(CTX_HEAD, None)
    return jax.shard_map(
        on_device,
        mesh=split,
        in_specs=(rows, rows, rows, P("head"), P("head")),
        out_specs=rows,
        check_vma=False,
    )
```

time: 82.7 us -> 64.2 us (0.78)
  blocking collectives: 13.2 us -> 36.4 us
  waiting for transfers between devices: 30.4 us -> 10.1 us
  matrix products: 12.1 us -> 0 us
  starting transfers between devices: 18.2 us -> 8.76 us
  Pallas kernels: 0 us -> 4.46 us
  other arithmetic: 2.1 us -> 0 us
  local copies, waits for them, and re-layouts: 6.01 us -> 4.26 us
    all_to_all x3 -> x0, waiting for transfers between devices: 30.4 us -> none  [the longest x1 14.5 us: on_device(): arrived = lax.all_to_all(packed, PEERS, 0, 0, tiled=True)]
    all_to_all x1 -> x2, blocking collectives: 13.2 us -> 36.4 us  [exchange(): return lax.all_to_all(value, PEERS, 0, 0, tiled=True)]
    all_to_all x3 -> x0, starting transfers between devices: 18.2 us -> none  [the longest x1 9.98 us: on_device(): arrived = lax.all_to_all(packed, PEERS, 0, 0, tiled=True)]
    dot_general x16 -> x0, matrix products: 12.1 us -> none  [the longest x4 4.48 us: on_device(): jnp.einsum('htd,hde->hte', direction, key_state, precision=HIGH)]
    ppermute x0 -> x6, waiting for transfers between devices: none -> 10.1 us  [from_ring(): lax.ppermute(value, axis, [(i, (i + step) % size) for i in range(size)])]
    ppermute x0 -> x6, starting transfers between devices: none -> 8.76 us  [from_ring(): lax.ppermute(value, axis, [(i, (i + step) % size) for i in range(size)])]
    pallas_call x0 -> x4, Pallas kernels: none -> 4.46 us  [the longest x1 2.88 us: on_device(): pl.pallas_call(functools.partial(solve_kernel, subs=subs, steps=steps_x),...]
    add x7 -> x0, other arithmetic: 1.15 us -> none  [the longest x1 0.9 us: earlier_states(): outgoing = column + jnp.where(ranks > y, local, 0.0)]
  transfers between devices with their start and end apart: 3 -> 6, of which waited for: 3 -> 6; matrix products, arithmetic and copies ran while one was open for 3% -> 0% of each run, Pallas kernels for 0% -> 0%
where the time goes in v2:
time: 64.2 us; the launch traced here: 64 us
  blocking collectives  36.4 us (57%)
  waiting for transfers between devices  10.1 us (16%)
  starting transfers between devices  8.76 us (14%)
  Pallas kernels  4.46 us (7%)
  local copies, waits for them, and re-layouts  4.26 us (7%)
    all_to_all x2, blocking collectives, exchange(): return lax.all_to_all(value, PEERS, 0, 0, tiled=True)  36.4 us
    ppermute x6, waiting for transfers between devices, from_ring(): lax.ppermute(value, axis, [(i, (i + step) % size) for i in range(size)])  10.1 us
    ppermute x6, starting transfers between devices, from_ring(): lax.ppermute(value, axis, [(i, (i + step) % size) for i in range(size)])  8.76 us
    unnamed x10, local copies, waits for them, and re-layouts  3.39 us
    pallas_call x1, Pallas kernels, on_device(): pl.pallas_call(functools.partial(solve_kernel, subs=subs, steps=steps_x),...  2.88 us
  transfers between devices with their start and end apart: 6, of which 6 were waited for; matrix products, arithmetic and copies ran while one was open for 0% of the time, Pallas kernels for 0%

profile of v2, /device:TPU:1, one launch (start us, length us, event | category | flops | bytes accessed | tf_op | source)
XLA Modules:
  0.0 64.0 jit_solution(10060104345511162337)
XLA Ops:
  0.0 0.0 copy-start.3
  0.0 0.0 copy-start.4
  0.0 0.7 %copy-done.3 = f32[256]{0:T(256)S(1)} copy-done((f32[256]{0:T(256)S(1)}, f32[256]{0:T(256)}, u32[]{:S(2)}) %copy-start.3) | copy-done | bytes 1048
  0.7 0.0 copy-done.4
  0.7 0.0 copy-start
  0.7 0.9 %copy-done = bf16[32,2048]{1,0:T(8,128)(2,1)S(1)} copy-done((bf16[32,2048]{1,0:T(8,128)(2,1)S(1)}, bf16[32,2048]{1,0:T(8,128)(2,1)}, u32[]{:S(2)}) %copy-start) | copy-done | bytes 131096
  1.6 0.0 copy-start.1
  1.6 0.9 %copy-done.1 = bf16[32,2048]{1,0:T(8,128)(2,1)S(1)} copy-done((bf16[32,2048]{1,0:T(8,128)(2,1)S(1)}, bf16[32,2048]{1,0:T(8,128)(2,1)}, u32[]{:S(2)}) %copy-start.1) | copy-done | bytes 131096
  2.5 0.0 copy-start.2
  2.5 0.9 %copy-done.2 = bf16[32,2048]{1,0:T(8,128)(2,1)S(1)} copy-done((bf16[32,2048]{1,0:T(8,128)(2,1)S(1)}, bf16[32,2048]{1,0:T(8,128)(2,1)}, u32[]{:S(2)}) %copy-start.2) | copy-done | bytes 131096
  3.4 1.2 %pack.1 = (bf16[16,3,32,128]{3,2,1,0:T(8,128)(2,1)S(1)}, f32[8,128]{1,0:T(8,128)S(1)}) custom-call(bf16[32,2048]{1,0:T(8,128)(2,1)S(1)} %copy-done, bf16[32,2048]{1,0:T(8,128)(2,1)S(1)} %copy-done.1, bf16[32,2048]{1,0:T(8,128)(2,1)S(1)} %copy-done.2, f32[2]{0:T(128)S(1)} %copy-done.4, f32[2,128]{1,0:T(2,128)S(1)} %bitcast.4), custom_call_target="tpu_custom_call" | custom-call | tf_op jit(solution)/shard_map/pack/pallas_call | solution.py:202
  4.6 22.2 %all_to_all.10.arrived_ref = bf16[16,3,32,128]{3,2,1,0:T(8,128)(2,1)S(1)} all-to-all(bf16[16,3,32,128]{3,2,1,0:T(8,128)(2,1)S(1)} %get-tuple-element.12), channel_id=1, replica_groups=mesh['x'=4,'y'=4,'core'=2,'head'=8] {'core','head'}, dimensions={0} | all-to-all | bytes 786432 | tf_op jit(solution)/shard_map/all_to_all | solution.py:181
  26.8 0.4 states.1
  27.2 3.0 %collective-permute-start.2 = (f32[128,256]{1,0:T(8,128)S(1)}, f32[128,256]{1,0:T(8,128)S(1)}, u32[]{:S(2)}, u32[]{:S(2)}) collective-permute-start(f32[128,256]{1,0:T(8,128)S(1)} %get-tuple-element.14.own_ref), channel_id=1, source_target_pairs={{0,32},{16,48},{32,0},{48,16},{1,33},{17,49},{33,1},{49,17},{2,34}... | collective-permute-start | bytes 393224 | tf_op jit(solution)/shard_map/ppermute | solution.py:187
  30.2 0.8 %collective-permute-start.1 = (f32[128,256]{1,0:T(8,128)S(1)}, f32[128,256]{1,0:T(8,128)S(1)}, u32[]{:S(2)}, u32[]{:S(2)}) collective-permute-start(f32[128,256]{1,0:T(8,128)S(1)} %get-tuple-element.14.own_ref), channel_id=1, source_target_pairs={{0,48},{16,0},{32,16},{48,32},{1,49},{17,1},{33,17},{49,33},{2,50}... | collective-permute-start | bytes 393224 | tf_op jit(solution)/shard_map/ppermute | solution.py:187
  30.9 0.7 %collective-permute-start = (f32[128,256]{1,0:T(8,128)S(1)}, f32[128,256]{1,0:T(8,128)S(1)}, u32[]{:S(2)}, u32[]{:S(2)}) collective-permute-start(f32[128,256]{1,0:T(8,128)S(1)} %get-tuple-element.14.own_ref), channel_id=1, source_target_pairs={{0,16},{16,32},{32,48},{48,0},{1,17},{17,33},{33,49},{49,1},{2,18}... | collective-permute-start | bytes 393224 | tf_op jit(solution)/shard_map/ppermute | solution.py:187
  31.6 0.9 %collective-permute-done.2.refs_2_ = f32[128,256]{1,0:T(8,128)S(1)} collective-permute-done((f32[128,256]{1,0:T(8,128)S(1)}, f32[128,256]{1,0:T(8,128)S(1)}, u32[]{:S(2)}, u32[]{:S(2)}) %collective-permute-start.2) | collective-permute-done | bytes 131104 | tf_op jit(solution)/shard_map/ppermute | solution.py:187
  32.6 3.1 %collective-permute-done.1.refs_1_ = f32[128,256]{1,0:T(8,128)S(1)} collective-permute-done((f32[128,256]{1,0:T(8,128)S(1)}, f32[128,256]{1,0:T(8,128)S(1)}, u32[]{:S(2)}, u32[]{:S(2)}) %collective-permute-start.1) | collective-permute-done | bytes 131104 | tf_op jit(solution)/shard_map/ppermute | solution.py:187
  35.7 0.3 collective-permute-done.refs_0_
  36.1 2.8 %collective-permute-start.5 = (f32[128,256]{1,0:T(8,128)S(1)}, f32[128,256]{1,0:T(8,128)S(1)}, u32[]{:S(2)}, u32[]{:S(2)}) collective-permute-start(f32[128,256]{1,0:T(8,128)S(1)} %get-tuple-element.16), channel_id=1, source_target_pairs={{0,128},{64,192},{128,0},{192,64},{1,129},{65,193},{129,1},{193,65... | collective-permute-start | bytes 393224 | tf_op jit(solution)/shard_map/ppermute | solution.py:187
  38.9 0.9 %collective-permute-start.4 = (f32[128,256]{1,0:T(8,128)S(1)}, f32[128,256]{1,0:T(8,128)S(1)}, u32[]{:S(2)}, u32[]{:S(2)}) collective-permute-start(f32[128,256]{1,0:T(8,128)S(1)} %get-tuple-element.16), channel_id=1, source_target_pairs={{0,192},{64,0},{128,64},{192,128},{1,193},{65,1},{129,65},{193,129... | collective-permute-start | bytes 393224 | tf_op jit(solution)/shard_map/ppermute | solution.py:187
  39.8 0.6 collective-permute-start.3
  40.4 1.1 %collective-permute-done.5.refs_2_ = f32[128,256]{1,0:T(8,128)S(1)} collective-permute-done((f32[128,256]{1,0:T(8,128)S(1)}, f32[128,256]{1,0:T(8,128)S(1)}, u32[]{:S(2)}, u32[]{:S(2)}) %collective-permute-start.5) | collective-permute-done | bytes 131104 | tf_op jit(solution)/shard_map/ppermute | solution.py:187
  41.5 1.5 %collective-permute-done.4.refs_1_ = f32[128,256]{1,0:T(8,128)S(1)} collective-permute-done((f32[128,256]{1,0:T(8,128)S(1)}, f32[128,256]{1,0:T(8,128)S(1)}, u32[]{:S(2)}, u32[]{:S(2)}) %collective-permute-start.4) | collective-permute-done | bytes 131104 | tf_op jit(solution)/shard_map/ppermute | solution.py:187
  43.0 3.1 %collective-permute-done.3.refs_0_ = f32[128,256]{1,0:T(8,128)S(1)} collective-permute-done((f32[128,256]{1,0:T(8,128)S(1)}, f32[128,256]{1,0:T(8,128)S(1)}, u32[]{:S(2)}, u32[]{:S(2)}) %collective-permute-start.3) | collective-permute-done | bytes 131104 | tf_op jit(solution)/shard_map/ppermute | solution.py:187
  46.1 2.9 %solve.1 = bf16[16,32,128]{2,1,0:T(8,128)(2,1)S(1)} custom-call(f32[8,128]{1,0:T(8,128)S(1)} %get-tuple-element.11.head_ref, bf16[16,3,32,128]{3,2,1,0:T(8,128)(2,1)S(1)} %all_to_all.10.arrived_ref, f32[3,128,256]{2,1,0:T(8,128)S(1)} %get-tuple-element.13.before_ref, f32[128,256]{1,0:T(8,128)S(1)} %get-tuple-element.15.earlier_ref, ...), custom_call_target="tpu_custom_call" | custom-call | tf_op jit(solution)/shard_map/solve/pallas_call | solution.py:236
  49.0 14.1 %all_to_all.11 = bf16[16,32,128]{2,1,0:T(8,128)(2,1)S(1)} all-to-all(bf16[16,32,128]{2,1,0:T(8,128)(2,1)S(1)} %solve.1), channel_id=1, replica_groups=mesh['x'=4,'y'=4,'core'=2,'head'=8] {'core','head'}, dimensions={0} | all-to-all | bytes 262144 | tf_op jit(solution)/shard_map/all_to_all | solution.py:181
  63.1 0.1 copy.6
  63.2 0.7 %reshape.11 = bf16[32,2048]{1,0:T(8,128)(2,1)} reshape(bf16[32,8,2,128]{3,2,1,0:T(2,128)(2,1)S(1)} %copy.6) | data formatting | bytes 262144 | tf_op jit(solution)/shard_map/reshape | solution.py:245
  (1 shorter events, 0.0 us)
Async XLA Ops:
  0.0 0.7 %copy-start.3 = (f32[256]{0:T(256)S(1)}, f32[256]{0:T(256)}, u32[]{:S(2)}) copy-start(f32[256]{0:T(256)} %param.9) | copy-start | bytes 3076
  0.0 0.7 %copy-start.4 = (f32[2]{0:T(128)S(1)}, f32[2]{0:T(128)}, u32[]{:S(2)}) copy-start(f32[2]{0:T(128)} %ridge_ref.1) | copy-start | bytes 28
  0.7 0.9 %copy-start = (bf16[32,2048]{1,0:T(8,128)(2,1)S(1)}, bf16[32,2048]{1,0:T(8,128)(2,1)}, u32[]{:S(2)}) copy-start(bf16[32,2048]{1,0:T(8,128)(2,1)} %query_ref.1) | copy-start | bytes 393220
  1.6 0.9 %copy-start.1 = (bf16[32,2048]{1,0:T(8,128)(2,1)S(1)}, bf16[32,2048]{1,0:T(8,128)(2,1)}, u32[]{:S(2)}) copy-start(bf16[32,2048]{1,0:T(8,128)(2,1)} %key_ref.1) | copy-start | bytes 393220
  2.5 0.9 %copy-start.2 = (bf16[32,2048]{1,0:T(8,128)(2,1)S(1)}, bf16[32,2048]{1,0:T(8,128)(2,1)}, u32[]{:S(2)}) copy-start(bf16[32,2048]{1,0:T(8,128)(2,1)} %value_ref.1) | copy-start | bytes 393220
  27.2 5.4 %collective-permute-start.2 = (f32[128,256]{1,0:T(8,128)S(1)}, f32[128,256]{1,0:T(8,128)S(1)}, u32[]{:S(2)}, u32[]{:S(2)}) collective-permute-start(f32[128,256]{1,0:T(8,128)S(1)} %get-tuple-element.14.own_ref), channel_id=1, source_target_pairs={{0,32},{16,48},{32,0},{48,16},{1,33},{17,49},{33,1},{49,17},{2,34}... | collective-permute-start | bytes 393224 | tf_op jit(solution)/shard_map/ppermute | solution.py:187
  30.2 5.6 %collective-permute-start.1 = (f32[128,256]{1,0:T(8,128)S(1)}, f32[128,256]{1,0:T(8,128)S(1)}, u32[]{:S(2)}, u32[]{:S(2)}) collective-permute-start(f32[128,256]{1,0:T(8,128)S(1)} %get-tuple-element.14.own_ref), channel_id=1, source_target_pairs={{0,48},{16,0},{32,16},{48,32},{1,49},{17,1},{33,17},{49,33},{2,50}... | collective-permute-start | bytes 393224 | tf_op jit(solution)/shard_map/ppermute | solution.py:187
  30.9 5.1 %collective-permute-start = (f32[128,256]{1,0:T(8,128)S(1)}, f32[128,256]{1,0:T(8,128)S(1)}, u32[]{:S(2)}, u32[]{:S(2)}) collective-permute-start(f32[128,256]{1,0:T(8,128)S(1)} %get-tuple-element.14.own_ref), channel_id=1, source_target_pairs={{0,16},{16,32},{32,48},{48,0},{1,17},{17,33},{33,49},{49,1},{2,18}... | collective-permute-start | bytes 393224 | tf_op jit(solution)/shard_map/ppermute | solution.py:187
  36.1 5.4 %collective-permute-start.5 = (f32[128,256]{1,0:T(8,128)S(1)}, f32[128,256]{1,0:T(8,128)S(1)}, u32[]{:S(2)}, u32[]{:S(2)}) collective-permute-start(f32[128,256]{1,0:T(8,128)S(1)} %get-tuple-element.16), channel_id=1, source_target_pairs={{0,128},{64,192},{128,0},{192,64},{1,129},{65,193},{129,1},{193,65... | collective-permute-start | bytes 393224 | tf_op jit(solution)/shard_map/ppermute | solution.py:187
  38.9 4.1 %collective-permute-start.4 = (f32[128,256]{1,0:T(8,128)S(1)}, f32[128,256]{1,0:T(8,128)S(1)}, u32[]{:S(2)}, u32[]{:S(2)}) collective-permute-start(f32[128,256]{1,0:T(8,128)S(1)} %get-tuple-element.16), channel_id=1, source_target_pairs={{0,192},{64,0},{128,64},{192,128},{1,193},{65,1},{129,65},{193,129... | collective-permute-start | bytes 393224 | tf_op jit(solution)/shard_map/ppermute | solution.py:187
  39.8 6.3 %collective-permute-start.3 = (f32[128,256]{1,0:T(8,128)S(1)}, f32[128,256]{1,0:T(8,128)S(1)}, u32[]{:S(2)}, u32[]{:S(2)}) collective-permute-start(f32[128,256]{1,0:T(8,128)S(1)} %get-tuple-element.16), channel_id=1, source_target_pairs={{0,64},{64,128},{128,192},{192,0},{1,65},{65,129},{129,193},{193,1... | collective-permute-start | bytes 393224 | tf_op jit(solution)/shard_map/ppermute | solution.py:187

commit v3 on v2

--- a/solution.py
+++ b/solution.py
@@ -53,23 +53,42 @@
 
 
 def pack_kernel(
-    query_ref, key_ref, value_ref, ridge_ref, gain_ref, out_ref, head_ref, held, flags, *, peers
+    query_ref, key_ref, value_ref, ridge_ref, gain_ref, out_ref, head_ref,
+    held, ridges, gains, flags, *, peers
 ):
+    half = peers // 2
     copies = [
-        pltpu.make_async_copy(ref, held.at[which], flags.at[which])
-        for which, ref in enumerate((query_ref, key_ref, value_ref))
+        pltpu.make_async_copy(source, target, flags.at[i])
+        for i, (source, target) in enumerate(
+            (
+                (query_ref, held.at[0]),
+                (key_ref, held.at[1]),
+                (value_ref, held.at[2]),
+                (ridge_ref, ridges),
+                (gain_ref, gains),
+            )
+        )
     ]
     for copy in copies:
         copy.start()
-    core = lax.axis_index("core")
-    head_ref[...] = jnp.full(head_ref.shape, ridge_ref[core], F32)
-    head_ref[pl.ds(0, 1), :] = gain_ref[pl.ds(core, 1), :]
-    half = peers // 2
-    for which, copy in enumerate(copies):
-        copy.wait()
+    for i in range(3):
+        copies[i].wait()
         for peer in range(peers):
             head = 2 * (peer % half) + peer // half
-            out_ref[peer, which] = held[which, :, head * DH : (head + 1) * DH]
+            out_ref[peer, i] = held[i, :, head * DH : (head + 1) * DH]
+    copies[3].wait()
+    copies[4].wait()
+    core = lax.axis_index("core")
+    head_ref[...] = jnp.full(head_ref.shape, ridges[core], F32)
+    head_ref[pl.ds(0, 1), :] = gains[pl.ds(core, 1), :]
+
+
+def unpack_kernel(arrived_ref, out_ref):
+    peers = arrived_ref.shape[0]
+    half = peers // 2
+    for peer in range(peers):
+        head = 2 * (peer % half) + peer // half
+        out_ref[:, head * DH : (head + 1) * DH] = arrived_ref[peer]
 
 
 def states_kernel(arrived_ref, before_ref, total_ref, *, subs):
@@ -189,7 +208,11 @@
 
 
 def ring_steps(size):
-    return sorted(range(1, size), key=lambda step: min(step, size - step))
+    return [size - 1] + list(range(1, size - 1))
+
+
+def in_hbm(value):
+    return pltpu.with_memory_space_constraint(value, pltpu.HBM)
 
 
 def on_device(queries, keys, values, ridge, gain):
@@ -205,15 +228,17 @@
             jax.ShapeDtypeStruct((peers, 3, rows, DH), BF),
             jax.ShapeDtypeStruct((8, DH), F32),
         ),
-        in_specs=[HBM, HBM, HBM, SMEM, VMEM],
+        in_specs=[HBM] * 5,
         out_specs=(VMEM, VMEM),
         scratch_shapes=[
             pltpu.VMEM((3, rows, columns), BF),
-            pltpu.SemaphoreType.DMA((3,)),
+            pltpu.SMEM((2,), F32),
+            pltpu.VMEM((2, DH), F32),
+            pltpu.SemaphoreType.DMA((5,)),
         ],
         compiler_params=ROOM,
         name="pack",
-    )(queries, keys, values, ridge, gain.reshape(2, DH))
+    )(*map(in_hbm, (queries, keys, values, ridge, gain.reshape(2, DH))))
     arrived = exchange(packed)
 
     state = jax.ShapeDtypeStruct((DH, 2 * DH), F32)
@@ -241,8 +266,14 @@
         compiler_params=ROOM,
         name="solve",
     )(head, arrived, before, earlier, *from_ring(total, "x", steps_x))
-    home = exchange(outgoing).reshape(2, half, rows, DH)
-    return home.transpose(2, 1, 0, 3).reshape(rows, columns)
+    return pl.pallas_call(
+        unpack_kernel,
+        out_shape=jax.ShapeDtypeStruct((rows, columns), BF),
+        in_specs=[VMEM],
+        out_specs=VMEM,
+        compiler_params=ROOM,
+        name="unpack",
+    )(exchange(outgoing))
 
 
 def solution(mesh):

time: 64.2 us -> 59.5 us (0.927)
  local copies, waits for them, and re-layouts: 4.26 us -> 0 us
  waiting for transfers between devices: 10.1 us -> 7.55 us
  starting transfers between devices: 8.76 us -> 11.2 us
  blocking collectives: 36.4 us -> 35.4 us
    unnamed x10 -> x0, local copies, waits for them, and re-layouts: 3.39 us -> none
    ppermute x6, waiting for transfers between devices: 10.1 us -> 7.55 us  [from_ring(): lax.ppermute(value, axis, [(i, (i + step) % size) for i in range(size)])]
    ppermute x6, starting transfers between devices: 8.76 us -> 11.2 us  [from_ring(): lax.ppermute(value, axis, [(i, (i + step) % size) for i in range(size)])]
    all_to_all x2, blocking collectives: 36.4 us -> 35.4 us  [exchange(): return lax.all_to_all(value, PEERS, 0, 0, tiled=True)]
    reshape x1 -> x0, local copies, waits for them, and re-layouts: 0.73 us -> none  [on_device(): return home.transpose(2, 1, 0, 3).reshape(rows, columns)]
    pallas_call x0 -> x1, Pallas kernels: none -> 0.68 us  [on_device(): pl.pallas_call(unpack_kernel, out_shape=jax.ShapeDtypeStruct((rows, colum...]
  transfers between devices with their start and end apart: 6 -> 6, of which waited for: 6 -> 2; matrix products, arithmetic and copies ran while one was open for 0% -> 0% of each run, Pallas kernels for 0% -> 0%
where the time goes in v3:
time: 59.5 us; the launch traced here: 59.3 us
  blocking collectives  35.4 us (59%)
  starting transfers between devices  11.2 us (19%)
  waiting for transfers between devices  7.55 us (13%)
  Pallas kernels  5.1 us (9%)
    all_to_all x2, blocking collectives, exchange(): return lax.all_to_all(value, PEERS, 0, 0, tiled=True)  35.4 us
    ppermute x6, starting transfers between devices, from_ring(): lax.ppermute(value, axis, [(i, (i + step) % size) for i in range(size)])  11.2 us
    ppermute x6, waiting for transfers between devices, from_ring(): lax.ppermute(value, axis, [(i, (i + step) % size) for i in range(size)])  7.55 us
    pallas_call x1, Pallas kernels, on_device(): pl.pallas_call(functools.partial(solve_kernel, subs=subs, steps=steps_x),...  2.88 us
  transfers between devices with their start and end apart: 6, of which 2 were waited for; matrix products, arithmetic and copies ran while one was open for 0% of the time, Pallas kernels for 0%

profile of v3, /device:TPU:1, one launch (start us, length us, event | category | flops | bytes accessed | tf_op | source)
XLA Modules:
  0.0 59.3 jit_solution(4758486882786454564)
XLA Ops:
  0.0 1.1 %pack.1 = (bf16[16,3,32,128]{3,2,1,0:T(8,128)(2,1)S(1)}, f32[8,128]{1,0:T(8,128)S(1)}) custom-call(bf16[32,2048]{1,0:T(8,128)(2,1)} %query_ref.1, bf16[32,2048]{1,0:T(8,128)(2,1)} %key_ref.1, bf16[32,2048]{1,0:T(8,128)(2,1)} %value_ref.1, f32[2]{0:T(128)} %ridge_ref.1, f32[2,128]{1,0:T(2,128)} %bitcast.1), custom_call_target="tpu_custom_call" | custom-call | tf_op jit(solution)/shard_map/pack/pallas_call | solution.py:225
  1.1 22.2 %all_to_all.10.arrived_ref = bf16[16,3,32,128]{3,2,1,0:T(8,128)(2,1)S(1)} all-to-all(bf16[16,3,32,128]{3,2,1,0:T(8,128)(2,1)S(1)} %get-tuple-element.12), channel_id=1, replica_groups=mesh['x'=4,'y'=4,'core'=2,'head'=8] {'core','head'}, dimensions={0} | all-to-all | bytes 786432 | tf_op jit(solution)/shard_map/all_to_all | solution.py:200
  23.3 0.4 states.1
  23.7 3.0 %collective-permute-start.2 = (f32[128,256]{1,0:T(8,128)S(1)}, f32[128,256]{1,0:T(8,128)S(1)}, u32[]{:S(2)}, u32[]{:S(2)}) collective-permute-start(f32[128,256]{1,0:T(8,128)S(1)} %get-tuple-element.14.own_ref), channel_id=1, source_target_pairs={{0,32},{16,48},{32,0},{48,16},{1,33},{17,49},{33,1},{49,17},{2,34}... | collective-permute-start | bytes 393224 | tf_op jit(solution)/shard_map/ppermute | solution.py:206
  26.7 0.4 collective-permute-start.1
  27.1 2.3 %collective-permute-start = (f32[128,256]{1,0:T(8,128)S(1)}, f32[128,256]{1,0:T(8,128)S(1)}, u32[]{:S(2)}, u32[]{:S(2)}) collective-permute-start(f32[128,256]{1,0:T(8,128)S(1)} %get-tuple-element.14.own_ref), channel_id=1, source_target_pairs={{0,48},{16,0},{32,16},{48,32},{1,49},{17,1},{33,17},{49,33},{2,50}... | collective-permute-start | bytes 393224 | tf_op jit(solution)/shard_map/ppermute | solution.py:206
  29.4 0.0 collective-permute-done.2.refs_2_
  29.4 3.5 %collective-permute-done.1.refs_1_ = f32[128,256]{1,0:T(8,128)S(1)} collective-permute-done((f32[128,256]{1,0:T(8,128)S(1)}, f32[128,256]{1,0:T(8,128)S(1)}, u32[]{:S(2)}, u32[]{:S(2)}) %collective-permute-start.1) | collective-permute-done | bytes 131104 | tf_op jit(solution)/shard_map/ppermute | solution.py:206
  32.9 0.0 collective-permute-done.refs_0_
  32.9 2.8 %collective-permute-start.5 = (f32[128,256]{1,0:T(8,128)S(1)}, f32[128,256]{1,0:T(8,128)S(1)}, u32[]{:S(2)}, u32[]{:S(2)}) collective-permute-start(f32[128,256]{1,0:T(8,128)S(1)} %get-tuple-element.16), channel_id=1, source_target_pairs={{0,128},{64,192},{128,0},{192,64},{1,129},{65,193},{129,1},{193,65... | collective-permute-start | bytes 393224 | tf_op jit(solution)/shard_map/ppermute | solution.py:206
  35.8 0.3 collective-permute-start.4
  36.1 2.4 %collective-permute-start.3 = (f32[128,256]{1,0:T(8,128)S(1)}, f32[128,256]{1,0:T(8,128)S(1)}, u32[]{:S(2)}, u32[]{:S(2)}) collective-permute-start(f32[128,256]{1,0:T(8,128)S(1)} %get-tuple-element.16), channel_id=1, source_target_pairs={{0,192},{64,0},{128,64},{192,128},{1,193},{65,1},{129,65},{193,129... | collective-permute-start | bytes 393224 | tf_op jit(solution)/shard_map/ppermute | solution.py:206
  38.4 0.0 collective-permute-done.5.refs_2_
  38.4 4.1 %collective-permute-done.4.refs_1_ = f32[128,256]{1,0:T(8,128)S(1)} collective-permute-done((f32[128,256]{1,0:T(8,128)S(1)}, f32[128,256]{1,0:T(8,128)S(1)}, u32[]{:S(2)}, u32[]{:S(2)}) %collective-permute-start.4) | collective-permute-done | bytes 131104 | tf_op jit(solution)/shard_map/ppermute | solution.py:206
  42.5 0.0 collective-permute-done.3.refs_0_
  42.5 2.9 %solve.1 = bf16[16,32,128]{2,1,0:T(8,128)(2,1)S(1)} custom-call(f32[8,128]{1,0:T(8,128)S(1)} %get-tuple-element.11.head_ref, bf16[16,3,32,128]{3,2,1,0:T(8,128)(2,1)S(1)} %all_to_all.10.arrived_ref, f32[3,128,256]{2,1,0:T(8,128)S(1)} %get-tuple-element.13.before_ref, f32[128,256]{1,0:T(8,128)S(1)} %get-tuple-element.15.earlier_ref, ...), custom_call_target="tpu_custom_call" | custom-call | tf_op jit(solution)/shard_map/solve/pallas_call | solution.py:261
  45.4 13.2 %all_to_all.11.arrived_ref = bf16[16,32,128]{2,1,0:T(8,128)(2,1)S(1)} all-to-all(bf16[16,32,128]{2,1,0:T(8,128)(2,1)S(1)} %solve.1), channel_id=1, replica_groups=mesh['x'=4,'y'=4,'core'=2,'head'=8] {'core','head'}, dimensions={0} | all-to-all | bytes 262144 | tf_op jit(solution)/shard_map/all_to_all | solution.py:200
  58.6 0.7 %unpack.1 = bf16[32,2048]{1,0:T(8,128)(2,1)} custom-call(bf16[16,32,128]{2,1,0:T(8,128)(2,1)S(1)} %all_to_all.11.arrived_ref), custom_call_target="tpu_custom_call" | custom-call | tf_op jit(solution)/shard_map/unpack/pallas_call | solution.py:269
  (1 shorter events, 0.0 us)
Async XLA Ops:
  23.7 5.7 %collective-permute-start.2 = (f32[128,256]{1,0:T(8,128)S(1)}, f32[128,256]{1,0:T(8,128)S(1)}, u32[]{:S(2)}, u32[]{:S(2)}) collective-permute-start(f32[128,256]{1,0:T(8,128)S(1)} %get-tuple-element.14.own_ref), channel_id=1, source_target_pairs={{0,32},{16,48},{32,0},{48,16},{1,33},{17,49},{33,1},{49,17},{2,34}... | collective-permute-start | bytes 393224 | tf_op jit(solution)/shard_map/ppermute | solution.py:206
  26.7 6.2 %collective-permute-start.1 = (f32[128,256]{1,0:T(8,128)S(1)}, f32[128,256]{1,0:T(8,128)S(1)}, u32[]{:S(2)}, u32[]{:S(2)}) collective-permute-start(f32[128,256]{1,0:T(8,128)S(1)} %get-tuple-element.14.own_ref), channel_id=1, source_target_pairs={{0,16},{16,32},{32,48},{48,0},{1,17},{17,33},{33,49},{49,1},{2,18}... | collective-permute-start | bytes 393224 | tf_op jit(solution)/shard_map/ppermute | solution.py:206
  27.1 5.8 %collective-permute-start = (f32[128,256]{1,0:T(8,128)S(1)}, f32[128,256]{1,0:T(8,128)S(1)}, u32[]{:S(2)}, u32[]{:S(2)}) collective-permute-start(f32[128,256]{1,0:T(8,128)S(1)} %get-tuple-element.14.own_ref), channel_id=1, source_target_pairs={{0,48},{16,0},{32,16},{48,32},{1,49},{17,1},{33,17},{49,33},{2,50}... | collective-permute-start | bytes 393224 | tf_op jit(solution)/shard_map/ppermute | solution.py:206
  32.9 5.5 %collective-permute-start.5 = (f32[128,256]{1,0:T(8,128)S(1)}, f32[128,256]{1,0:T(8,128)S(1)}, u32[]{:S(2)}, u32[]{:S(2)}) collective-permute-start(f32[128,256]{1,0:T(8,128)S(1)} %get-tuple-element.16), channel_id=1, source_target_pairs={{0,128},{64,192},{128,0},{192,64},{1,129},{65,193},{129,1},{193,65... | collective-permute-start | bytes 393224 | tf_op jit(solution)/shard_map/ppermute | solution.py:206
  35.8 6.7 %collective-permute-start.4 = (f32[128,256]{1,0:T(8,128)S(1)}, f32[128,256]{1,0:T(8,128)S(1)}, u32[]{:S(2)}, u32[]{:S(2)}) collective-permute-start(f32[128,256]{1,0:T(8,128)S(1)} %get-tuple-element.16), channel_id=1, source_target_pairs={{0,64},{64,128},{128,192},{192,0},{1,65},{65,129},{129,193},{193,1... | collective-permute-start | bytes 393224 | tf_op jit(solution)/shard_map/ppermute | solution.py:206
  36.1 6.4 %collective-permute-start.3 = (f32[128,256]{1,0:T(8,128)S(1)}, f32[128,256]{1,0:T(8,128)S(1)}, u32[]{:S(2)}, u32[]{:S(2)}) collective-permute-start(f32[128,256]{1,0:T(8,128)S(1)} %get-tuple-element.16), channel_id=1, source_target_pairs={{0,192},{64,0},{128,64},{192,128},{1,193},{65,1},{129,65},{193,129... | collective-permute-start | bytes 393224 | tf_op jit(solution)/shard_map/ppermute | solution.py:206

commit v4 on v3

--- a/solution.py
+++ b/solution.py
@@ -14,6 +14,7 @@
 EPS = 1e-06
 DH = 128
 SUB = 128
+HALF = DH // 2
 
 VMEM = pl.BlockSpec(memory_space=pltpu.VMEM)
 HBM = pl.BlockSpec(memory_space=pltpu.HBM)
@@ -91,6 +92,21 @@
         out_ref[:, head * DH : (head + 1) * DH] = arrived_ref[peer]
 
 
+def without_mirror(state):
+    key_state, value_state = state[:, :DH], state[:, DH:]
+    corner = key_state[HALF:, HALF:]
+    return tall(
+        [value_state, key_state[:HALF], wide([corner[: HALF // 2], corner[HALF // 2 :]])]
+    )
+
+
+def with_mirror(rows):
+    upper, corner = rows[DH : DH + HALF], rows[DH + HALF :]
+    corner = tall([corner[:, :HALF], corner[:, HALF:]])
+    lower = wide([upper[:, HALF:].T, corner])
+    return tall([upper, lower]), rows[:DH]
+
+
 def states_kernel(arrived_ref, before_ref, total_ref, *, subs):
     total = None
     for sub in range(subs):
@@ -104,7 +120,7 @@
         total = state if total is None else total + state
         if sub + 1 < subs:
             before_ref[sub] = total
-    total_ref[...] = total
+    total_ref[...] = without_mirror(total)
 
 
 def from_others(index, own, others, steps):
@@ -126,72 +142,99 @@
     earlier_ref[...] = earlier
 
 
-def solve_kernel(head_ref, arrived_ref, before_ref, earlier_ref, *refs, subs, steps):
+def prepare_kernel(
+    arrived_ref, query_ref, key_t_ref, weight_ref, unit_ref, parts_ref, image_ref, *, subs
+):
+    row = lax.broadcasted_iota(jnp.int32, (SUB, SUB), 0)
+    column = lax.broadcasted_iota(jnp.int32, (SUB, SUB), 1)
+    causal = column <= row
+    for sub in range(subs):
+        key = tokens_of(arrived_ref, 1, sub)
+        key_f = key.astype(F32)
+        unit = lax.rsqrt(jnp.sum((key_f * key_f).T, 0, keepdims=True) + EPS)
+        weight = jnp.where(causal, unit * unit, 0.0)
+        unit_ref[sub] = jnp.where(causal, unit, 0.0)
+        weight_ref[sub] = weight
+        key_t = key_f.T.astype(BF)
+        key_t_ref[sub] = key_t
+        query = tokens_of(arrived_ref, 0, sub).astype(F32)
+        query = query * lax.rsqrt(squared_sum(query) + EPS)
+        query_ref[sub] = query
+        parts = wide(pieces(query, 3))
+        parts_ref[sub] = parts
+        scores = dot(parts, tall([key_t] * 3)) * weight
+        image_ref[sub] = dot(wide(pieces(scores, 2)), tall([key, key]))
+
+
+def solve_kernel(
+    head_ref, arrived_ref, before_ref, earlier_ref, query_ref, key_t_ref, weight_ref, unit_ref,
+    parts_ref, image_ref, *refs, subs, steps
+):
     out_ref = refs[-1]
     gain, strength = head_ref[0:1, :], head_ref[1:2, :]
     earlier = earlier_ref[...]
     _, rows_before = from_others(lax.axis_index("x"), earlier, refs[:-1], steps)
-    base = earlier + rows_before
-    row = lax.broadcasted_iota(jnp.int32, (SUB, SUB), 0)
-    column = lax.broadcasted_iota(jnp.int32, (SUB, SUB), 1)
-    causal = column <= row
+    key_base, value_base = with_mirror(earlier + rows_before)
 
     every = range(subs)
-    keys, key_pair, operator, low_state, weights, units = [], [], [], [], [], []
-    value_state = []
+    key_pair, operator, low_state, value_state = [], [], [], []
     resid, answer, direction, rr_now = [], [], [], []
     for sub in every:
-        state = base if sub == 0 else base + before_ref[sub - 1]
+        key_state, value = key_base, value_base
+        if sub > 0:
+            key_state = key_state + before_ref[sub - 1, :, :DH]
+            value = value + before_ref[sub - 1, :, DH:]
+        high, middle, low = pieces(key_state, 3)
         key = tokens_of(arrived_ref, 1, sub)
-        key_f = key.astype(F32)
-        unit_t = lax.rsqrt(jnp.sum((key_f * key_f).T, 0, keepdims=True) + EPS)
-        units.append(jnp.where(causal, unit_t, 0.0))
-        weights.append(jnp.where(causal, unit_t * unit_t, 0.0))
-        high, middle, low = pieces(state[:, :DH], 3)
-        key_t = key_f.T.astype(BF)
-        keys.append(key_t)
         key_pair.append(tall([key, key]))
-        operator.append(tall([wide([key_t, high])] * 3))
-        low_state.append(tall([wide([middle, low])] * 2))
-        value_state.append(state[:, DH:])
-        query = tokens_of(arrived_ref, 0, sub).astype(F32)
-        query = query * lax.rsqrt(squared_sum(query) + EPS)
+        line = wide([key_t_ref[sub], high])
+        operator.append(tall([line, line, line, wide([jnp.zeros_like(high), middle])]))
+        low_state.append(tall([middle, low]))
+        value_state.append(value)
+        query = query_ref[sub]
         resid.append(query)
         direction.append(query)
         answer.append(None)
         rr_now.append(squared_sum(query))
+    def one_turn(s, turn):
+        if turn == 0:
+            p = [parts_ref[s, :, i * DH : (i + 1) * DH] for i in range(3)]
+            image = dot(wide(p + p[:1]), operator[s][:, SUB:]) + image_ref[s]
+        else:
+            p = pieces(direction[s], 3)
+            first = dot(wide(p + p[:1]), operator[s])
+            scores = wide(pieces(first[:, :SUB] * weight_ref[s], 2))
+            image = dot(scores, key_pair[s]) + first[:, SUB:]
+        image = image + dot(wide([p[1], p[0]]), low_state[s]) + strength * direction[s]
+        alpha = rr_now[s] / (jnp.sum(direction[s] * image, -1, keepdims=True) + EPS)
+        step = alpha * direction[s]
+        answer[s] = step if turn == 0 else answer[s] + step
+        if turn + 1 < ITERS:
+            resid[s] = resid[s] - alpha * image
+            rr_next = squared_sum(resid[s])
+            direction[s] = resid[s] + rr_next / (rr_now[s] + EPS) * direction[s]
+            rr_now[s] = rr_next
+
     for turn in range(ITERS):
-        parts = [wide(pieces(direction[s], 3)) for s in every]
-        first = [dot(parts[s], operator[s]) for s in every]
-        rest = [dot(parts[s][:, : 2 * DH], low_state[s]) for s in every]
-        scores = [wide(pieces(first[s][:, :SUB] * weights[s], 2)) for s in every]
-        image = [
-            dot(scores[s], key_pair[s])
-            + (first[s][:, SUB:] + (rest[s][:, :DH] + rest[s][:, DH:]))
-            + strength * direction[s]
-            for s in every
-        ]
         for s in every:
-            alpha = rr_now[s] / (jnp.sum(direction[s] * image[s], -1, keepdims=True) + EPS)
-            step = alpha * direction[s]
-            answer[s] = step if turn == 0 else answer[s] + step
-            if turn + 1 < ITERS:
-                resid[s] = resid[s] - alpha * image[s]
-                rr_next = squared_sum(resid[s])
-                direction[s] = resid[s] + rr_next / (rr_now[s] + EPS) * direction[s]
-                rr_now[s] = rr_next
+            one_turn(s, turn)
+    parts = [wide(pieces(answer[s], 2)) for s in every]
+    split = [pieces(value_state[s], 2) for s in every]
+    first = [
+        dot(parts[s], tall([wide([key_t_ref[s], split[s][0]])] * 2)) for s in every
+    ]
+    rest = [dot(parts[s][:, :DH], split[s][1]) for s in every]
+    scores = [wide(pieces(first[s][:, :SUB] * unit_ref[s], 2)) for s in every]
+    values = [tokens_of(arrived_ref, 2, s) for s in every]
+    readout = [
+        dot(scores[s], tall([values[s], values[s]])) + (first[s][:, SUB:] + rest[s])
+        for s in every
+    ]
     rows = out_ref.shape[1]
     count = SUB // rows
     for s in every:
-        high, low = pieces(value_state[s], 2)
-        parts = wide(pieces(answer[s], 2))
-        first = dot(parts, tall([wide([keys[s], high])] * 2))
-        scores = wide(pieces(first[:, :SUB] * units[s], 2))
-        value = tokens_of(arrived_ref, 2, s)
-        readout = dot(scores, tall([value, value]))
-        readout = readout + (first[:, SUB:] + dot(parts[:, :DH], low))
-        scale = lax.rsqrt(squared_sum(readout) * (1.0 / DH) + EPS)
-        normed = (readout * scale * gain).astype(BF)
+        scale = lax.rsqrt(squared_sum(readout[s]) * (1.0 / DH) + EPS)
+        normed = (readout[s] * scale * gain).astype(BF)
         for i in range(count):
             out_ref[s * count + i] = normed[i * rows : (i + 1) * rows]
 
@@ -241,10 +284,10 @@
     )(*map(in_hbm, (queries, keys, values, ridge, gain.reshape(2, DH))))
     arrived = exchange(packed)
 
-    state = jax.ShapeDtypeStruct((DH, 2 * DH), F32)
+    state = jax.ShapeDtypeStruct((DH + HALF + HALF // 2, DH), F32)
     before, own = pl.pallas_call(
         functools.partial(states_kernel, subs=subs),
-        out_shape=(jax.ShapeDtypeStruct((subs - 1,) + state.shape, F32), state),
+        out_shape=(jax.ShapeDtypeStruct((subs - 1, DH, 2 * DH), F32), state),
         in_specs=[VMEM],
         out_specs=(VMEM, VMEM),
         compiler_params=ROOM,
@@ -258,14 +301,30 @@
         compiler_params=ROOM,
         name="row",
     )(own, *from_ring(own, "y", steps_y))
+    square = (subs, SUB, DH)
+    prepared = pl.pallas_call(
+        functools.partial(prepare_kernel, subs=subs),
+        out_shape=(
+            jax.ShapeDtypeStruct(square, F32),
+            jax.ShapeDtypeStruct(square, BF),
+            jax.ShapeDtypeStruct(square, F32),
+            jax.ShapeDtypeStruct(square, F32),
+            jax.ShapeDtypeStruct((subs, SUB, 3 * DH), BF),
+            jax.ShapeDtypeStruct(square, F32),
+        ),
+        in_specs=[VMEM],
+        out_specs=(VMEM,) * 6,
+        compiler_params=ROOM,
+        name="prepare",
+    )(arrived)
     outgoing = pl.pallas_call(
         functools.partial(solve_kernel, subs=subs, steps=steps_x),
         out_shape=jax.ShapeDtypeStruct((peers, rows, DH), BF),
-        in_specs=[VMEM] * (3 + n_x),
+        in_specs=[VMEM] * (9 + n_x),
         out_specs=VMEM,
         compiler_params=ROOM,
         name="solve",
-    )(head, arrived, before, earlier, *from_ring(total, "x", steps_x))
+    )(head, arrived, before, earlier, *prepared, *from_ring(total, "x", steps_x))
     return pl.pallas_call(
         unpack_kernel,
         out_shape=jax.ShapeDtypeStruct((rows, columns), BF),

time: 59.5 us -> 58.5 us (0.983)
  waiting for transfers between devices: 7.55 us -> 5.2 us
  Pallas kernels: 5.1 us -> 5.95 us
    ppermute x6, waiting for transfers between devices: 7.55 us -> 5.2 us  [from_ring(): lax.ppermute(value, axis, [(i, (i + step) % size) for i in range(size)])]
    pallas_call x0 -> x1, Pallas kernels: none -> 0.9 us  [on_device(): pl.pallas_call(functools.partial(prepare_kernel, subs=subs), out_shape=(j...]
  transfers between devices with their start and end apart: 6 -> 6, of which waited for: 2 -> 3; matrix products, arithmetic and copies ran while one was open for 0% -> 0% of each run, Pallas kernels for 0% -> 2%
where the time goes in v4:
time: 58.5 us; the launch traced here: 57.9 us
  blocking collectives  35.6 us (61%)
  starting transfers between devices  11.1 us (19%)
  Pallas kernels  5.95 us (10%)
  waiting for transfers between devices  5.2 us (9%)
    all_to_all x2, blocking collectives, exchange(): return lax.all_to_all(value, PEERS, 0, 0, tiled=True)  35.6 us
    ppermute x6, starting transfers between devices, from_ring(): lax.ppermute(value, axis, [(i, (i + step) % size) for i in range(size)])  11.1 us
    ppermute x6, waiting for transfers between devices, from_ring(): lax.ppermute(value, axis, [(i, (i + step) % size) for i in range(size)])  5.2 us
    pallas_call x1, Pallas kernels, on_device(): pl.pallas_call(functools.partial(solve_kernel, subs=subs, steps=steps_x),...  2.77 us
  transfers between devices with their start and end apart: 6, of which 3 were waited for; matrix products, arithmetic and copies ran while one was open for 0% of the time, Pallas kernels for 2%

profile of v4, /device:TPU:1, one launch (start us, length us, event | category | flops | bytes accessed | tf_op | source)
XLA Modules:
  0.0 57.9 jit_solution(7601872794862289363)
XLA Ops:
  0.0 1.1 %pack.1 = (bf16[16,3,32,128]{3,2,1,0:T(8,128)(2,1)S(1)}, f32[8,128]{1,0:T(8,128)S(1)}) custom-call(bf16[32,2048]{1,0:T(8,128)(2,1)} %query_ref.1, bf16[32,2048]{1,0:T(8,128)(2,1)} %key_ref.1, bf16[32,2048]{1,0:T(8,128)(2,1)} %value_ref.1, f32[2]{0:T(128)} %ridge_ref.1, f32[2,128]{1,0:T(2,128)} %bitcast.1), custom_call_target="tpu_custom_call" | custom-call | tf_op jit(solution)/shard_map/pack/pallas_call | solution.py:268
  1.1 22.2 %all_to_all.10.arrived_ref = bf16[16,3,32,128]{3,2,1,0:T(8,128)(2,1)S(1)} all-to-all(bf16[16,3,32,128]{3,2,1,0:T(8,128)(2,1)S(1)} %get-tuple-element.18), channel_id=1, replica_groups=mesh['x'=4,'y'=4,'core'=2,'head'=8] {'core','head'}, dimensions={0} | all-to-all | bytes 786432 | tf_op jit(solution)/shard_map/all_to_all | solution.py:243
  23.3 0.4 states.1
  23.8 3.0 %collective-permute-start.2 = (f32[224,128]{1,0:T(8,128)S(1)}, f32[224,128]{1,0:T(8,128)S(1)}, u32[]{:S(2)}, u32[]{:S(2)}) collective-permute-start(f32[224,128]{1,0:T(8,128)S(1)} %get-tuple-element.20.own_ref), channel_id=1, source_target_pairs={{0,32},{16,48},{32,0},{48,16},{1,33},{17,49},{33,1},{49,17},{2,34}... | collective-permute-start | bytes 344072 | tf_op jit(solution)/shard_map/ppermute | solution.py:249
  26.7 0.4 collective-permute-start.1
  27.1 2.3 %collective-permute-start = (f32[224,128]{1,0:T(8,128)S(1)}, f32[224,128]{1,0:T(8,128)S(1)}, u32[]{:S(2)}, u32[]{:S(2)}) collective-permute-start(f32[224,128]{1,0:T(8,128)S(1)} %get-tuple-element.20.own_ref), channel_id=1, source_target_pairs={{0,48},{16,0},{32,16},{48,32},{1,49},{17,1},{33,17},{49,33},{2,50}... | collective-permute-start | bytes 344072 | tf_op jit(solution)/shard_map/ppermute | solution.py:249
  29.4 0.0 collective-permute-done.2.refs_2_
  29.4 2.6 %collective-permute-done.1.refs_1_ = f32[224,128]{1,0:T(8,128)S(1)} collective-permute-done((f32[224,128]{1,0:T(8,128)S(1)}, f32[224,128]{1,0:T(8,128)S(1)}, u32[]{:S(2)}, u32[]{:S(2)}) %collective-permute-start.1) | collective-permute-done | bytes 114720 | tf_op jit(solution)/shard_map/ppermute | solution.py:249
  32.0 0.3 collective-permute-done.refs_0_
  32.3 2.8 %collective-permute-start.5 = (f32[224,128]{1,0:T(8,128)S(1)}, f32[224,128]{1,0:T(8,128)S(1)}, u32[]{:S(2)}, u32[]{:S(2)}) collective-permute-start(f32[224,128]{1,0:T(8,128)S(1)} %get-tuple-element.28), channel_id=1, source_target_pairs={{0,128},{64,192},{128,0},{192,64},{1,129},{65,193},{129,1},{193,65... | collective-permute-start | bytes 344072 | tf_op jit(solution)/shard_map/ppermute | solution.py:249
  35.2 0.3 collective-permute-start.4
  35.5 2.4 %collective-permute-start.3 = (f32[224,128]{1,0:T(8,128)S(1)}, f32[224,128]{1,0:T(8,128)S(1)}, u32[]{:S(2)}, u32[]{:S(2)}) collective-permute-start(f32[224,128]{1,0:T(8,128)S(1)} %get-tuple-element.28), channel_id=1, source_target_pairs={{0,192},{64,0},{128,64},{192,128},{1,193},{65,1},{129,65},{193,129... | collective-permute-start | bytes 344072 | tf_op jit(solution)/shard_map/ppermute | solution.py:249
  37.8 0.9 %prepare.1 = (f32[4,128,128]{2,1,0:T(8,128)S(1)}, bf16[4,128,128]{2,1,0:T(8,128)(2,1)S(1)}, f32[4,128,128]{2,1,0:T(8,128)S(1)}, f32[4,128,128]{2,1,0:T(8,128)S(1...) custom-call(bf16[16,3,32,128]{3,2,1,0:T(8,128)(2,1)S(1)} %all_to_all.10.arrived_ref), custom_call_target="tpu_custom_call" | custom-call | tf_op jit(solution)/shard_map/prepare/pallas_call | solution.py:305
  38.8 0.0 collective-permute-done.5.refs_2_
  38.8 2.3 %collective-permute-done.4.refs_1_ = f32[224,128]{1,0:T(8,128)S(1)} collective-permute-done((f32[224,128]{1,0:T(8,128)S(1)}, f32[224,128]{1,0:T(8,128)S(1)}, u32[]{:S(2)}, u32[]{:S(2)}) %collective-permute-start.4) | collective-permute-done | bytes 114720 | tf_op jit(solution)/shard_map/ppermute | solution.py:249
  41.1 0.0 collective-permute-done.3.refs_0_
  41.1 2.8 %solve.1 = bf16[16,32,128]{2,1,0:T(8,128)(2,1)S(1)} custom-call(f32[8,128]{1,0:T(8,128)S(1)} %get-tuple-element.17.head_ref, bf16[16,3,32,128]{3,2,1,0:T(8,128)(2,1)S(1)} %all_to_all.10.arrived_ref, f32[3,128,256]{2,1,0:T(8,128)S(1)} %get-tuple-element.19.before_ref, f32[224,128]{1,0:T(8,128)S(1)} %get-tuple-element.21.earlier_ref, ...), custom_call_target="tpu_custom_call" | custom-call | tf_op jit(solution)/shard_map/solve/pallas_call | solution.py:320
  43.9 13.4 %all_to_all.11.arrived_ref = bf16[16,32,128]{2,1,0:T(8,128)(2,1)S(1)} all-to-all(bf16[16,32,128]{2,1,0:T(8,128)(2,1)S(1)} %solve.1), channel_id=1, replica_groups=mesh['x'=4,'y'=4,'core'=2,'head'=8] {'core','head'}, dimensions={0} | all-to-all | bytes 262144 | tf_op jit(solution)/shard_map/all_to_all | solution.py:243
  57.2 0.7 %unpack.1 = bf16[32,2048]{1,0:T(8,128)(2,1)} custom-call(bf16[16,32,128]{2,1,0:T(8,128)(2,1)S(1)} %all_to_all.11.arrived_ref), custom_call_target="tpu_custom_call" | custom-call | tf_op jit(solution)/shard_map/unpack/pallas_call | solution.py:328
  (1 shorter events, 0.0 us)
Async XLA Ops:
  23.8 5.6 %collective-permute-start.2 = (f32[224,128]{1,0:T(8,128)S(1)}, f32[224,128]{1,0:T(8,128)S(1)}, u32[]{:S(2)}, u32[]{:S(2)}) collective-permute-start(f32[224,128]{1,0:T(8,128)S(1)} %get-tuple-element.20.own_ref), channel_id=1, source_target_pairs={{0,32},{16,48},{32,0},{48,16},{1,33},{17,49},{33,1},{49,17},{2,34}... | collective-permute-start | bytes 344072 | tf_op jit(solution)/shard_map/ppermute | solution.py:249
  26.7 5.2 %collective-permute-start.1 = (f32[224,128]{1,0:T(8,128)S(1)}, f32[224,128]{1,0:T(8,128)S(1)}, u32[]{:S(2)}, u32[]{:S(2)}) collective-permute-start(f32[224,128]{1,0:T(8,128)S(1)} %get-tuple-element.20.own_ref), channel_id=1, source_target_pairs={{0,16},{16,32},{32,48},{48,0},{1,17},{17,33},{33,49},{49,1},{2,18}... | collective-permute-start | bytes 344072 | tf_op jit(solution)/shard_map/ppermute | solution.py:249
  27.1 5.2 %collective-permute-start = (f32[224,128]{1,0:T(8,128)S(1)}, f32[224,128]{1,0:T(8,128)S(1)}, u32[]{:S(2)}, u32[]{:S(2)}) collective-permute-start(f32[224,128]{1,0:T(8,128)S(1)} %get-tuple-element.20.own_ref), channel_id=1, source_target_pairs={{0,48},{16,0},{32,16},{48,32},{1,49},{17,1},{33,17},{49,33},{2,50}... | collective-permute-start | bytes 344072 | tf_op jit(solution)/shard_map/ppermute | solution.py:249
  32.3 6.4 %collective-permute-start.5 = (f32[224,128]{1,0:T(8,128)S(1)}, f32[224,128]{1,0:T(8,128)S(1)}, u32[]{:S(2)}, u32[]{:S(2)}) collective-permute-start(f32[224,128]{1,0:T(8,128)S(1)} %get-tuple-element.28), channel_id=1, source_target_pairs={{0,128},{64,192},{128,0},{192,64},{1,129},{65,193},{129,1},{193,65... | collective-permute-start | bytes 344072 | tf_op jit(solution)/shard_map/ppermute | solution.py:249
  35.2 5.9 %collective-permute-start.4 = (f32[224,128]{1,0:T(8,128)S(1)}, f32[224,128]{1,0:T(8,128)S(1)}, u32[]{:S(2)}, u32[]{:S(2)}) collective-permute-start(f32[224,128]{1,0:T(8,128)S(1)} %get-tuple-element.28), channel_id=1, source_target_pairs={{0,64},{64,128},{128,192},{192,0},{1,65},{65,129},{129,193},{193,1... | collective-permute-start | bytes 344072 | tf_op jit(solution)/shard_map/ppermute | solution.py:249
  35.5 5.6 %collective-permute-start.3 = (f32[224,128]{1,0:T(8,128)S(1)}, f32[224,128]{1,0:T(8,128)S(1)}, u32[]{:S(2)}, u32[]{:S(2)}) collective-permute-start(f32[224,128]{1,0:T(8,128)S(1)} %get-tuple-element.28), channel_id=1, source_target_pairs={{0,192},{64,0},{128,64},{192,128},{1,193},{65,1},{129,65},{193,129... | collective-permute-start | bytes 344072 | tf_op jit(solution)/shard_map/ppermute | solution.py:249

commit v5 on v4

--- a/solution.py
+++ b/solution.py
@@ -123,23 +123,27 @@
     total_ref[...] = without_mirror(total)
 
 
-def from_others(index, own, others, steps):
+def ring_places():
+    core, x, y = lax.axis_index("core"), lax.axis_index("x"), lax.axis_index("y")
+    return core == 0, jnp.where(core == 0, y, x), jnp.where(core == 0, x, y)
+
+
+def gather_kernel(own_ref, *refs, steps, size):
+    count = len(steps)
+    others, sends, keep_ref = refs[:count], refs[count:-1], refs[-1]
+    later_steps = [1, 3, 2]
+    by_row, first, second = ring_places()
+    own = own_ref[...]
     total, earlier = own, None
     for step, ref in zip(steps, others):
         value = ref[...]
         total = total + value
-        part = jnp.where(index >= step, value, 0.0)
+        part = jnp.where(first >= step, value, 0.0)
         earlier = part if earlier is None else earlier + part
-    return total, earlier
-
-
-def row_kernel(own_ref, *refs, steps):
-    total_ref, earlier_ref = refs[-2:]
-    total, earlier = from_others(
-        lax.axis_index("y"), own_ref[...], refs[:-2], steps
-    )
-    total_ref[...] = total
-    earlier_ref[...] = earlier
+    keep_ref[...] = earlier
+    both = earlier + own
+    for step, ref in zip(later_steps, sends):
+        ref[...] = jnp.where(by_row, total, jnp.where(second + step < size, both, earlier))
 
 
 def prepare_kernel(
@@ -172,9 +176,12 @@
 ):
     out_ref = refs[-1]
     gain, strength = head_ref[0:1, :], head_ref[1:2, :]
+    by_row, _, second = ring_places()
     earlier = earlier_ref[...]
-    _, rows_before = from_others(lax.axis_index("x"), earlier, refs[:-1], steps)
-    key_base, value_base = with_mirror(earlier + rows_before)
+    for step, ref in zip(steps, refs[:-1]):
+        taken = jnp.logical_or(jnp.logical_not(by_row), second >= step)
+        earlier = earlier + jnp.where(taken, ref[...], 0.0)
+    key_base, value_base = with_mirror(earlier)
 
     every = range(subs)
     key_pair, operator, low_state, value_state = [], [], [], []
@@ -243,15 +250,27 @@
     return lax.all_to_all(value, PEERS, 0, 0, tiled=True)
 
 
-def from_ring(value, axis, steps):
-    size = lax.axis_size(axis)
-    return [
-        lax.ppermute(value, axis, [(i, (i + step) % size) for i in range(size)]) for step in steps
-    ]
+def from_ring(values, steps, size, stage):
+    def place(x, y, core):
+        return (x * size + y) * 2 + core
+
+    def pairs(step):
+        out = []
+        for x in range(size):
+            for y in range(size):
+                for core in range(2):
+                    along_y = core == stage
+                    to_x = x if along_y else (x + step) % size
+                    to_y = (y + step) % size if along_y else y
+                    out.append((place(x, y, core), place(to_x, to_y, core)))
+        return out
+
+    axes = ("x", "y", "core")
+    return [lax.ppermute(value, axes, pairs(step)) for value, step in zip(values, steps)]
 
 
 def ring_steps(size):
-    return [size - 1] + list(range(1, size - 1))
+    return [3, 1, 2]
 
 
 def in_hbm(value):
@@ -262,9 +281,9 @@
     rows, columns = queries.shape
     half = lax.axis_size("head")
     peers = 2 * half
-    n_x, n_y = lax.axis_size("x"), lax.axis_size("y")
+    size = lax.axis_size("x")
     subs = peers * rows // SUB
-    steps_x, steps_y = ring_steps(n_x), ring_steps(n_y)
+    steps = ring_steps(size)
     packed, head = pl.pallas_call(
         functools.partial(pack_kernel, peers=peers),
         out_shape=(
@@ -293,14 +312,6 @@
         compiler_params=ROOM,
         name="states",
     )(arrived)
-    total, earlier = pl.pallas_call(
-        functools.partial(row_kernel, steps=steps_y),
-        out_shape=(state, state),
-        in_specs=[VMEM] * n_y,
-        out_specs=(VMEM, VMEM),
-        compiler_params=ROOM,
-        name="row",
-    )(own, *from_ring(own, "y", steps_y))
     square = (subs, SUB, DH)
     prepared = pl.pallas_call(
         functools.partial(prepare_kernel, subs=subs),
@@ -317,14 +328,25 @@
         compiler_params=ROOM,
         name="prepare",
     )(arrived)
+    around, prepared = lax.optimization_barrier(
+        (from_ring([own] * len(steps), steps, size, 0), prepared)
+    )
+    *sends, keep = pl.pallas_call(
+        functools.partial(gather_kernel, steps=steps, size=size),
+        out_shape=(state,) * size,
+        in_specs=[VMEM] * size,
+        out_specs=(VMEM,) * size,
+        compiler_params=ROOM,
+        name="gather",
+    )(own, *around)
     outgoing = pl.pallas_call(
-        functools.partial(solve_kernel, subs=subs, steps=steps_x),
+        functools.partial(solve_kernel, subs=subs, steps=[1, 3, 2]),
         out_shape=jax.ShapeDtypeStruct((peers, rows, DH), BF),
-        in_specs=[VMEM] * (9 + n_x),
+        in_specs=[VMEM] * (9 + size),
         out_specs=VMEM,
         compiler_params=ROOM,
         name="solve",
-    )(head, arrived, before, earlier, *prepared, *from_ring(total, "x", steps_x))
+    )(head, arrived, before, keep, *prepared, *from_ring(sends, [1, 3, 2], size, 1))
     return pl.pallas_call(
         unpack_kernel,
         out_shape=jax.ShapeDtypeStruct((rows, columns), BF),

time: 58.5 us -> 58.4 us (level)
  blocking collectives: 35.6 us -> 37.4 us
  starting transfers between devices: 11.1 us -> 9.92 us
    all_to_all x2, blocking collectives: 35.6 us -> 37.4 us  [exchange(): return lax.all_to_all(value, PEERS, 0, 0, tiled=True)]
    ppermute x6, starting transfers between devices: 11.1 us -> 9.92 us  [from_ring(): lax.ppermute(value, axes, pairs(step))]
where the time goes in v5:
time: 58.4 us; the launch traced here: 58.2 us
  blocking collectives  37.4 us (64%)
  starting transfers between devices  9.92 us (17%)
  Pallas kernels  5.98 us (10%)
  waiting for transfers between devices  4.85 us (8%)
    all_to_all x2, blocking collectives, exchange(): return lax.all_to_all(value, PEERS, 0, 0, tiled=True)  37.4 us
    ppermute x6, starting transfers between devices, from_ring(): lax.ppermute(value, axes, pairs(step))  9.92 us
    ppermute x6, waiting for transfers between devices, from_ring(): lax.ppermute(value, axes, pairs(step))  4.85 us
    pallas_call x1, Pallas kernels, on_device(): pl.pallas_call(functools.partial(solve_kernel, subs=subs, steps=[1, 3, 2]...  2.77 us
  transfers between devices with their start and end apart: 6, of which 3 were waited for; matrix products, arithmetic and copies ran while one was open for 0% of the time, Pallas kernels for 2%

profile of v5, /device:TPU:1, one launch (start us, length us, event | category | flops | bytes accessed | tf_op | source)
XLA Modules:
  0.0 58.2 jit_solution(836153984146843882)
XLA Ops:
  0.0 1.1 %pack.1 = (bf16[16,3,32,128]{3,2,1,0:T(8,128)(2,1)S(1)}, f32[8,128]{1,0:T(8,128)S(1)}) custom-call(bf16[32,2048]{1,0:T(8,128)(2,1)} %query_ref.1, bf16[32,2048]{1,0:T(8,128)(2,1)} %key_ref.1, bf16[32,2048]{1,0:T(8,128)(2,1)} %value_ref.1, f32[2]{0:T(128)} %ridge_ref.1, f32[2,128]{1,0:T(2,128)} %bitcast.1), custom_call_target="tpu_custom_call" | custom-call | tf_op jit(solution)/shard_map/pack/pallas_call | solution.py:287
  1.1 22.2 %all_to_all.10.arrived_ref = bf16[16,3,32,128]{3,2,1,0:T(8,128)(2,1)S(1)} all-to-all(bf16[16,3,32,128]{3,2,1,0:T(8,128)(2,1)S(1)} %get-tuple-element.29), channel_id=1, replica_groups=mesh['x'=4,'y'=4,'core'=2,'head'=8] {'core','head'}, dimensions={0} | all-to-all | bytes 786432 | tf_op jit(solution)/shard_map/all_to_all | solution.py:250
  23.3 0.4 states.1
  23.8 2.8 %collective-permute-start.2 = (f32[224,128]{1,0:T(8,128)S(1)}, f32[224,128]{1,0:T(8,128)S(1)}, u32[]{:S(2)}, u32[]{:S(2)}) collective-permute-start(f32[224,128]{1,0:T(8,128)S(1)} %get-tuple-element.31.own_ref), channel_id=1, source_target_pairs={{0,32},{8,136},{16,48},{24,152},{32,0},{40,168},{48,16},{56,184},{... | collective-permute-start | bytes 344072 | tf_op jit(solution)/shard_map/ppermute | solution.py:269
  26.6 0.3 collective-permute-start.1
  26.9 2.4 %collective-permute-start = (f32[224,128]{1,0:T(8,128)S(1)}, f32[224,128]{1,0:T(8,128)S(1)}, u32[]{:S(2)}, u32[]{:S(2)}) collective-permute-start(f32[224,128]{1,0:T(8,128)S(1)} %get-tuple-element.31.own_ref), channel_id=1, source_target_pairs={{0,48},{8,200},{16,0},{24,216},{32,16},{40,232},{48,32},{56,248},{... | collective-permute-start | bytes 344072 | tf_op jit(solution)/shard_map/ppermute | solution.py:269
  29.2 0.9 %prepare.1 = (f32[4,128,128]{2,1,0:T(8,128)S(1)}, bf16[4,128,128]{2,1,0:T(8,128)(2,1)S(1)}, f32[4,128,128]{2,1,0:T(8,128)S(1)}, f32[4,128,128]{2,1,0:T(8,128)S(1...) custom-call(bf16[16,3,32,128]{3,2,1,0:T(8,128)(2,1)S(1)} %all_to_all.10.arrived_ref), custom_call_target="tpu_custom_call" | custom-call | tf_op jit(solution)/shard_map/prepare/pallas_call | solution.py:316
  30.1 0.0 collective-permute-done.2.refs_2_
  30.2 1.3 %collective-permute-done.1.refs_1_ = f32[224,128]{1,0:T(8,128)S(1)} collective-permute-done((f32[224,128]{1,0:T(8,128)S(1)}, f32[224,128]{1,0:T(8,128)S(1)}, u32[]{:S(2)}, u32[]{:S(2)}) %collective-permute-start.1) | collective-permute-done | bytes 114720 | tf_op jit(solution)/shard_map/ppermute | solution.py:269
  31.4 0.0 collective-permute-done.refs_0_
  31.4 0.1 gather.1
  31.5 1.4 %collective-permute-start.3 = (f32[224,128]{1,0:T(8,128)S(1)}, f32[224,128]{1,0:T(8,128)S(1)}, u32[]{:S(2)}, u32[]{:S(2)}) collective-permute-start(f32[224,128]{1,0:T(8,128)S(1)} %get-tuple-element.48), channel_id=1, source_target_pairs={{0,64},{8,24},{16,80},{24,40},{32,96},{40,56},{48,112},{56,8},{64,... | collective-permute-start | bytes 344072 | tf_op jit(solution)/shard_map/ppermute | solution.py:269
  32.9 1.5 %collective-permute-start.4 = (f32[224,128]{1,0:T(8,128)S(1)}, f32[224,128]{1,0:T(8,128)S(1)}, u32[]{:S(2)}, u32[]{:S(2)}) collective-permute-start(f32[224,128]{1,0:T(8,128)S(1)} %get-tuple-element.49), channel_id=1, source_target_pairs={{0,192},{8,56},{16,208},{24,8},{32,224},{40,24},{48,240},{56,40},{... | collective-permute-start | bytes 344072 | tf_op jit(solution)/shard_map/ppermute | solution.py:269
  34.4 1.6 %collective-permute-start.5 = (f32[224,128]{1,0:T(8,128)S(1)}, f32[224,128]{1,0:T(8,128)S(1)}, u32[]{:S(2)}, u32[]{:S(2)}) collective-permute-start(f32[224,128]{1,0:T(8,128)S(1)} %get-tuple-element.50), channel_id=1, source_target_pairs={{0,128},{8,40},{16,144},{24,56},{32,160},{40,8},{48,176},{56,24},{... | collective-permute-start | bytes 344072 | tf_op jit(solution)/shard_map/ppermute | solution.py:269
  36.0 0.5 collective-permute-done.3.refs_0_
  36.5 0.0 collective-permute-done.4.refs_1_
  36.5 3.0 %collective-permute-done.5.refs_2_ = f32[224,128]{1,0:T(8,128)S(1)} collective-permute-done((f32[224,128]{1,0:T(8,128)S(1)}, f32[224,128]{1,0:T(8,128)S(1)}, u32[]{:S(2)}, u32[]{:S(2)}) %collective-permute-start.5) | collective-permute-done | bytes 114720 | tf_op jit(solution)/shard_map/ppermute | solution.py:269
  39.6 2.8 %solve.1 = bf16[16,32,128]{2,1,0:T(8,128)(2,1)S(1)} custom-call(f32[8,128]{1,0:T(8,128)S(1)} %get-tuple-element.28.head_ref, bf16[16,3,32,128]{3,2,1,0:T(8,128)(2,1)S(1)} %all_to_all.10.arrived_ref, f32[3,128,256]{2,1,0:T(8,128)S(1)} %get-tuple-element.30.before_ref, f32[224,128]{1,0:T(8,128)S(1)} %get-tuple-element.41.earlier_ref, ...), custom_call_target="tpu_custom_call" | custom-call | tf_op jit(solution)/shard_map/solve/pallas_call | solution.py:342
  42.3 15.2 %all_to_all.11.arrived_ref = bf16[16,32,128]{2,1,0:T(8,128)(2,1)S(1)} all-to-all(bf16[16,32,128]{2,1,0:T(8,128)(2,1)S(1)} %solve.1), channel_id=1, replica_groups=mesh['x'=4,'y'=4,'core'=2,'head'=8] {'core','head'}, dimensions={0} | all-to-all | bytes 262144 | tf_op jit(solution)/shard_map/all_to_all | solution.py:250
  57.6 0.7 %unpack.1 = bf16[32,2048]{1,0:T(8,128)(2,1)} custom-call(bf16[16,32,128]{2,1,0:T(8,128)(2,1)S(1)} %all_to_all.11.arrived_ref), custom_call_target="tpu_custom_call" | custom-call | tf_op jit(solution)/shard_map/unpack/pallas_call | solution.py:350
Async XLA Ops:
  23.8 6.4 %collective-permute-start.2 = (f32[224,128]{1,0:T(8,128)S(1)}, f32[224,128]{1,0:T(8,128)S(1)}, u32[]{:S(2)}, u32[]{:S(2)}) collective-permute-start(f32[224,128]{1,0:T(8,128)S(1)} %get-tuple-element.31.own_ref), channel_id=1, source_target_pairs={{0,32},{8,136},{16,48},{24,152},{32,0},{40,168},{48,16},{56,184},{... | collective-permute-start | bytes 344072 | tf_op jit(solution)/shard_map/ppermute | solution.py:269
  26.6 4.9 %collective-permute-start.1 = (f32[224,128]{1,0:T(8,128)S(1)}, f32[224,128]{1,0:T(8,128)S(1)}, u32[]{:S(2)}, u32[]{:S(2)}) collective-permute-start(f32[224,128]{1,0:T(8,128)S(1)} %get-tuple-element.31.own_ref), channel_id=1, source_target_pairs={{0,16},{8,72},{16,32},{24,88},{32,48},{40,104},{48,0},{56,120},{64... | collective-permute-start | bytes 344072 | tf_op jit(solution)/shard_map/ppermute | solution.py:269
  26.9 4.5 %collective-permute-start = (f32[224,128]{1,0:T(8,128)S(1)}, f32[224,128]{1,0:T(8,128)S(1)}, u32[]{:S(2)}, u32[]{:S(2)}) collective-permute-start(f32[224,128]{1,0:T(8,128)S(1)} %get-tuple-element.31.own_ref), channel_id=1, source_target_pairs={{0,48},{8,200},{16,0},{24,216},{32,16},{40,232},{48,32},{56,248},{... | collective-permute-start | bytes 344072 | tf_op jit(solution)/shard_map/ppermute | solution.py:269
  31.5 5.0 %collective-permute-start.3 = (f32[224,128]{1,0:T(8,128)S(1)}, f32[224,128]{1,0:T(8,128)S(1)}, u32[]{:S(2)}, u32[]{:S(2)}) collective-permute-start(f32[224,128]{1,0:T(8,128)S(1)} %get-tuple-element.48), channel_id=1, source_target_pairs={{0,64},{8,24},{16,80},{24,40},{32,96},{40,56},{48,112},{56,8},{64,... | collective-permute-start | bytes 344072 | tf_op jit(solution)/shard_map/ppermute | solution.py:269
  32.9 3.6 %collective-permute-start.4 = (f32[224,128]{1,0:T(8,128)S(1)}, f32[224,128]{1,0:T(8,128)S(1)}, u32[]{:S(2)}, u32[]{:S(2)}) collective-permute-start(f32[224,128]{1,0:T(8,128)S(1)} %get-tuple-element.49), channel_id=1, source_target_pairs={{0,192},{8,56},{16,208},{24,8},{32,224},{40,24},{48,240},{56,40},{... | collective-permute-start | bytes 344072 | tf_op jit(solution)/shard_map/ppermute | solution.py:269
  34.4 5.1 %collective-permute-start.5 = (f32[224,128]{1,0:T(8,128)S(1)}, f32[224,128]{1,0:T(8,128)S(1)}, u32[]{:S(2)}, u32[]{:S(2)}) collective-permute-start(f32[224,128]{1,0:T(8,128)S(1)} %get-tuple-element.50), channel_id=1, source_target_pairs={{0,128},{8,40},{16,144},{24,56},{32,160},{40,8},{48,176},{56,24},{... | collective-permute-start | bytes 344072 | tf_op jit(solution)/shard_map/ppermute | solution.py:269

commit v6 on v5

--- a/solution.py
+++ b/solution.py
@@ -107,19 +107,20 @@
     return tall([upper, lower]), rows[:DH]
 
 
-def states_kernel(arrived_ref, before_ref, total_ref, *, subs):
-    total = None
-    for sub in range(subs):
-        key = tokens_of(arrived_ref, 1, sub)
-        value = tokens_of(arrived_ref, 2, sub)
-        key_f = key.astype(F32)
-        unit = lax.rsqrt(squared_sum(key_f) + EPS)
-        right = wide([key_f * (unit * unit), value.astype(F32) * unit])
-        key_t = key_f.T.astype(BF)
-        state = dot(wide([key_t, key_t]), tall(pieces(right, 2)))
-        total = state if total is None else total + state
-        if sub + 1 < subs:
-            before_ref[sub] = total
+def state_of(arrived_ref, sub):
+    key_f = tokens_of(arrived_ref, 1, sub).astype(F32)
+    unit = lax.rsqrt(squared_sum(key_f) + EPS)
+    right = wide(
+        [key_f * (unit * unit), tokens_of(arrived_ref, 2, sub).astype(F32) * unit]
+    )
+    key_t = key_f.T.astype(BF)
+    return dot(wide([key_t, key_t]), tall(pieces(right, 2)))
+
+
+def states_kernel(arrived_ref, total_ref, *, subs):
+    total = state_of(arrived_ref, 0)
+    for sub in range(1, subs):
+        total = total + state_of(arrived_ref, sub)
     total_ref[...] = without_mirror(total)
 
 
@@ -147,12 +148,18 @@
 
 
 def prepare_kernel(
-    arrived_ref, query_ref, key_t_ref, weight_ref, unit_ref, parts_ref, image_ref, *, subs
+    arrived_ref, before_ref, query_ref, key_t_ref, weight_ref, unit_ref, parts_ref, image_ref,
+    *, subs
 ):
     row = lax.broadcasted_iota(jnp.int32, (SUB, SUB), 0)
     column = lax.broadcasted_iota(jnp.int32, (SUB, SUB), 1)
     causal = column <= row
+    total = None
     for sub in range(subs):
+        if sub + 1 < subs:
+            state = state_of(arrived_ref, sub)
+            total = state if sub == 0 else total + state
+            before_ref[sub] = total
         key = tokens_of(arrived_ref, 1, sub)
         key_f = key.astype(F32)
         unit = lax.rsqrt(jnp.sum((key_f * key_f).T, 0, keepdims=True) + EPS)
@@ -304,18 +311,19 @@
     arrived = exchange(packed)
 
     state = jax.ShapeDtypeStruct((DH + HALF + HALF // 2, DH), F32)
-    before, own = pl.pallas_call(
+    own = pl.pallas_call(
         functools.partial(states_kernel, subs=subs),
-        out_shape=(jax.ShapeDtypeStruct((subs - 1, DH, 2 * DH), F32), state),
+        out_shape=state,
         in_specs=[VMEM],
-        out_specs=(VMEM, VMEM),
+        out_specs=VMEM,
         compiler_params=ROOM,
         name="states",
     )(arrived)
     square = (subs, SUB, DH)
-    prepared = pl.pallas_call(
+    before, *prepared = pl.pallas_call(
         functools.partial(prepare_kernel, subs=subs),
         out_shape=(
+            jax.ShapeDtypeStruct((subs - 1, DH, 2 * DH), F32),
             jax.ShapeDtypeStruct(square, F32),
             jax.ShapeDtypeStruct(square, BF),
             jax.ShapeDtypeStruct(square, F32),
@@ -324,7 +332,7 @@
             jax.ShapeDtypeStruct(square, F32),
         ),
         in_specs=[VMEM],
-        out_specs=(VMEM,) * 6,
+        out_specs=(VMEM,) * 7,
         compiler_params=ROOM,
         name="prepare",
     )(arrived)

time: 58.4 us -> 58.4 us (level)
  no operation moved by 1% of the time
where the time goes in v6:
time: 58.4 us; the launch traced here: 58.2 us
  blocking collectives  37.4 us (64%)
  starting transfers between devices  9.92 us (17%)
  Pallas kernels  6.01 us (10%)
  waiting for transfers between devices  4.83 us (8%)
    all_to_all x2, blocking collectives, exchange(): return lax.all_to_all(value, PEERS, 0, 0, tiled=True)  37.4 us
    ppermute x6, starting transfers between devices, from_ring(): lax.ppermute(value, axes, pairs(step))  9.92 us
    ppermute x6, waiting for transfers between devices, from_ring(): lax.ppermute(value, axes, pairs(step))  4.83 us
    pallas_call x1, Pallas kernels, on_device(): pl.pallas_call(functools.partial(solve_kernel, subs=subs, steps=[1, 3, 2]...  2.78 us
  transfers between devices with their start and end apart: 6, of which 3 were waited for; matrix products, arithmetic and copies ran while one was open for 0% of the time, Pallas kernels for 2%

profile of v6, /device:TPU:1, one launch (start us, length us, event | category | flops | bytes accessed | tf_op | source)
XLA Modules:
  0.0 58.2 jit_solution(2615865995745329053)
XLA Ops:
  0.0 1.1 %pack.1 = (bf16[16,3,32,128]{3,2,1,0:T(8,128)(2,1)S(1)}, f32[8,128]{1,0:T(8,128)S(1)}) custom-call(bf16[32,2048]{1,0:T(8,128)(2,1)} %query_ref.1, bf16[32,2048]{1,0:T(8,128)(2,1)} %key_ref.1, bf16[32,2048]{1,0:T(8,128)(2,1)} %value_ref.1, f32[2]{0:T(128)} %ridge_ref.1, f32[2,128]{1,0:T(2,128)} %bitcast.1), custom_call_target="tpu_custom_call" | custom-call | tf_op jit(solution)/shard_map/pack/pallas_call | solution.py:294
  1.1 22.2 %all_to_all.10.arrived_ref = bf16[16,3,32,128]{3,2,1,0:T(8,128)(2,1)S(1)} all-to-all(bf16[16,3,32,128]{3,2,1,0:T(8,128)(2,1)S(1)} %get-tuple-element.28), channel_id=1, replica_groups=mesh['x'=4,'y'=4,'core'=2,'head'=8] {'core','head'}, dimensions={0} | all-to-all | bytes 786432 | tf_op jit(solution)/shard_map/all_to_all | solution.py:257
  23.3 0.4 states.1.own_ref
  23.8 2.8 %collective-permute-start.2 = (f32[224,128]{1,0:T(8,128)S(1)}, f32[224,128]{1,0:T(8,128)S(1)}, u32[]{:S(2)}, u32[]{:S(2)}) collective-permute-start(f32[224,128]{1,0:T(8,128)S(1)} %states.1.own_ref), channel_id=1, source_target_pairs={{0,32},{8,136},{16,48},{24,152},{32,0},{40,168},{48,16},{56,184},{... | collective-permute-start | bytes 344072 | tf_op jit(solution)/shard_map/ppermute | solution.py:276
  26.6 0.3 collective-permute-start.1
  26.9 2.4 %collective-permute-start = (f32[224,128]{1,0:T(8,128)S(1)}, f32[224,128]{1,0:T(8,128)S(1)}, u32[]{:S(2)}, u32[]{:S(2)}) collective-permute-start(f32[224,128]{1,0:T(8,128)S(1)} %states.1.own_ref), channel_id=1, source_target_pairs={{0,48},{8,200},{16,0},{24,216},{32,16},{40,232},{48,32},{56,248},{... | collective-permute-start | bytes 344072 | tf_op jit(solution)/shard_map/ppermute | solution.py:276
  29.2 0.9 %prepare.1 = (f32[3,128,256]{2,1,0:T(8,128)S(1)}, f32[4,128,128]{2,1,0:T(8,128)S(1)}, bf16[4,128,128]{2,1,0:T(8,128)(2,1)S(1)}, f32[4,128,128]{2,1,0:T(8,128)S(1...) custom-call(bf16[16,3,32,128]{3,2,1,0:T(8,128)(2,1)S(1)} %all_to_all.10.arrived_ref), custom_call_target="tpu_custom_call" | custom-call | tf_op jit(solution)/shard_map/prepare/pallas_call | solution.py:323
  30.2 0.0 collective-permute-done.2.refs_2_
  30.2 1.2 %collective-permute-done.1.refs_1_ = f32[224,128]{1,0:T(8,128)S(1)} collective-permute-done((f32[224,128]{1,0:T(8,128)S(1)}, f32[224,128]{1,0:T(8,128)S(1)}, u32[]{:S(2)}, u32[]{:S(2)}) %collective-permute-start.1) | collective-permute-done | bytes 114720 | tf_op jit(solution)/shard_map/ppermute | solution.py:276
  31.4 0.0 collective-permute-done.refs_0_
  31.4 0.1 gather.1
  31.5 1.4 %collective-permute-start.3 = (f32[224,128]{1,0:T(8,128)S(1)}, f32[224,128]{1,0:T(8,128)S(1)}, u32[]{:S(2)}, u32[]{:S(2)}) collective-permute-start(f32[224,128]{1,0:T(8,128)S(1)} %get-tuple-element.46), channel_id=1, source_target_pairs={{0,64},{8,24},{16,80},{24,40},{32,96},{40,56},{48,112},{56,8},{64,... | collective-permute-start | bytes 344072 | tf_op jit(solution)/shard_map/ppermute | solution.py:276
  32.9 1.5 %collective-permute-start.4 = (f32[224,128]{1,0:T(8,128)S(1)}, f32[224,128]{1,0:T(8,128)S(1)}, u32[]{:S(2)}, u32[]{:S(2)}) collective-permute-start(f32[224,128]{1,0:T(8,128)S(1)} %get-tuple-element.47), channel_id=1, source_target_pairs={{0,192},{8,56},{16,208},{24,8},{32,224},{40,24},{48,240},{56,40},{... | collective-permute-start | bytes 344072 | tf_op jit(solution)/shard_map/ppermute | solution.py:276
  34.4 1.6 %collective-permute-start.5 = (f32[224,128]{1,0:T(8,128)S(1)}, f32[224,128]{1,0:T(8,128)S(1)}, u32[]{:S(2)}, u32[]{:S(2)}) collective-permute-start(f32[224,128]{1,0:T(8,128)S(1)} %get-tuple-element.48), channel_id=1, source_target_pairs={{0,128},{8,40},{16,144},{24,56},{32,160},{40,8},{48,176},{56,24},{... | collective-permute-start | bytes 344072 | tf_op jit(solution)/shard_map/ppermute | solution.py:276
  36.0 0.5 collective-permute-done.3.refs_0_
  36.5 0.0 collective-permute-done.4.refs_1_
  36.5 3.0 %collective-permute-done.5.refs_2_ = f32[224,128]{1,0:T(8,128)S(1)} collective-permute-done((f32[224,128]{1,0:T(8,128)S(1)}, f32[224,128]{1,0:T(8,128)S(1)}, u32[]{:S(2)}, u32[]{:S(2)}) %collective-permute-start.5) | collective-permute-done | bytes 114720 | tf_op jit(solution)/shard_map/ppermute | solution.py:276
  39.6 2.8 %solve.1 = bf16[16,32,128]{2,1,0:T(8,128)(2,1)S(1)} custom-call(f32[8,128]{1,0:T(8,128)S(1)} %get-tuple-element.27.head_ref, bf16[16,3,32,128]{3,2,1,0:T(8,128)(2,1)S(1)} %all_to_all.10.arrived_ref, f32[3,128,256]{2,1,0:T(8,128)S(1)} %get-tuple-element.29.before_ref, f32[224,128]{1,0:T(8,128)S(1)} %get-tuple-element.39.earlier_ref, ...), custom_call_target="tpu_custom_call" | custom-call | tf_op jit(solution)/shard_map/solve/pallas_call | solution.py:350
  42.3 15.2 %all_to_all.11.arrived_ref = bf16[16,32,128]{2,1,0:T(8,128)(2,1)S(1)} all-to-all(bf16[16,32,128]{2,1,0:T(8,128)(2,1)S(1)} %solve.1), channel_id=1, replica_groups=mesh['x'=4,'y'=4,'core'=2,'head'=8] {'core','head'}, dimensions={0} | all-to-all | bytes 262144 | tf_op jit(solution)/shard_map/all_to_all | solution.py:257
  57.6 0.7 %unpack.1 = bf16[32,2048]{1,0:T(8,128)(2,1)} custom-call(bf16[16,32,128]{2,1,0:T(8,128)(2,1)S(1)} %all_to_all.11.arrived_ref), custom_call_target="tpu_custom_call" | custom-call | tf_op jit(solution)/shard_map/unpack/pallas_call | solution.py:358
Async XLA Ops:
  23.8 6.4 %collective-permute-start.2 = (f32[224,128]{1,0:T(8,128)S(1)}, f32[224,128]{1,0:T(8,128)S(1)}, u32[]{:S(2)}, u32[]{:S(2)}) collective-permute-start(f32[224,128]{1,0:T(8,128)S(1)} %states.1.own_ref), channel_id=1, source_target_pairs={{0,32},{8,136},{16,48},{24,152},{32,0},{40,168},{48,16},{56,184},{... | collective-permute-start | bytes 344072 | tf_op jit(solution)/shard_map/ppermute | solution.py:276
  26.6 4.9 %collective-permute-start.1 = (f32[224,128]{1,0:T(8,128)S(1)}, f32[224,128]{1,0:T(8,128)S(1)}, u32[]{:S(2)}, u32[]{:S(2)}) collective-permute-start(f32[224,128]{1,0:T(8,128)S(1)} %states.1.own_ref), channel_id=1, source_target_pairs={{0,16},{8,72},{16,32},{24,88},{32,48},{40,104},{48,0},{56,120},{64... | collective-permute-start | bytes 344072 | tf_op jit(solution)/shard_map/ppermute | solution.py:276
  26.9 4.5 %collective-permute-start = (f32[224,128]{1,0:T(8,128)S(1)}, f32[224,128]{1,0:T(8,128)S(1)}, u32[]{:S(2)}, u32[]{:S(2)}) collective-permute-start(f32[224,128]{1,0:T(8,128)S(1)} %states.1.own_ref), channel_id=1, source_target_pairs={{0,48},{8,200},{16,0},{24,216},{32,16},{40,232},{48,32},{56,248},{... | collective-permute-start | bytes 344072 | tf_op jit(solution)/shard_map/ppermute | solution.py:276
  31.5 5.0 %collective-permute-start.3 = (f32[224,128]{1,0:T(8,128)S(1)}, f32[224,128]{1,0:T(8,128)S(1)}, u32[]{:S(2)}, u32[]{:S(2)}) collective-permute-start(f32[224,128]{1,0:T(8,128)S(1)} %get-tuple-element.46), channel_id=1, source_target_pairs={{0,64},{8,24},{16,80},{24,40},{32,96},{40,56},{48,112},{56,8},{64,... | collective-permute-start | bytes 344072 | tf_op jit(solution)/shard_map/ppermute | solution.py:276
  32.9 3.6 %collective-permute-start.4 = (f32[224,128]{1,0:T(8,128)S(1)}, f32[224,128]{1,0:T(8,128)S(1)}, u32[]{:S(2)}, u32[]{:S(2)}) collective-permute-start(f32[224,128]{1,0:T(8,128)S(1)} %get-tuple-element.47), channel_id=1, source_target_pairs={{0,192},{8,56},{16,208},{24,8},{32,224},{40,24},{48,240},{56,40},{... | collective-permute-start | bytes 344072 | tf_op jit(solution)/shard_map/ppermute | solution.py:276
  34.4 5.1 %collective-permute-start.5 = (f32[224,128]{1,0:T(8,128)S(1)}, f32[224,128]{1,0:T(8,128)S(1)}, u32[]{:S(2)}, u32[]{:S(2)}) collective-permute-start(f32[224,128]{1,0:T(8,128)S(1)} %get-tuple-element.48), channel_id=1, source_target_pairs={{0,128},{8,40},{16,144},{24,56},{32,160},{40,8},{48,176},{56,24},{... | collective-permute-start | bytes 344072 | tf_op jit(solution)/shard_map/ppermute | solution.py:276
